TPU v7x, 512 devices: a whole 4x4x16 slice. The times are simulated.
512 devices in a mesh: row: 32 (over x, y, core), col: 16 (over z).
Axes of the slice: x: 4, y: 4, z: 16, core: 2. Of those that a mesh axis runs over, the one named last changes fastest.
Arguments:
- matrix: float32 [1, 8192, 2, 4096], P(None, 'row', None, 'col'), as said below
Outputs:
- updated: float32 [1, 8192, 2, 4096], P(None, 'row', None, 'col')
Inputs may be any that keep to these rules, and one draw needn't show every extreme that they name: matrix is symmetric, and its leading 3 * 256 rows and columns form a positive definite block.
All inputs are finite; a program needn't handle non-finite values.
Results may differ from a plain program's by a relative error of at most 0.0001.
Values sent between devices are 32-bit elements; how exact they have to be, the bound alone decides.
No kernel may reach another device: no remote copies, remote signals or barrier semaphores. Data moves between devices by JAX's collectives and lax.ppermute only.
A program may use at most 64 MiB of HBM per device.

v0:
```python
import jax
import jax.numpy as jnp
from jax import lax
from jax.sharding import PartitionSpec as P

PANELS = 3


def broadcast(array, axis, root):
    mine = lax.axis_index(axis) == root
    return lax.psum(jnp.where(mine, array, jnp.zeros_like(array)), axis)


def shards(matrix):
    blocks_r, width, blocks_c, _ = matrix.shape
    rows_n = lax.axis_size("row")
    cols_n = lax.axis_size("col")
    ratio = rows_n // cols_n
    my_row = lax.axis_index("row")
    my_col = lax.axis_index("col")
    glob_r = jnp.arange(blocks_r) * rows_n + my_row
    glob_c = jnp.arange(blocks_c) * cols_n + my_col
    current = matrix
    for panel in range(PANELS):
        i_own = panel // rows_n
        j_own = panel // cols_n
        corner = broadcast(current[i_own, :, j_own, :], "row", panel % rows_n)
        factor = jnp.linalg.cholesky(corner)
        source = current[:, :, j_own, :]
        stacked = source.transpose(2, 0, 1).reshape(width, blocks_r * width)
        solved = jax.scipy.linalg.solve_triangular(factor, stacked, lower=True)
        below = solved.reshape(width, blocks_r, width).transpose(1, 2, 0)
        sel_r = glob_r[:, None, None]
        column_vals = jnp.where(sel_r > panel, below, jnp.where(sel_r == panel, factor[None], 0.0))
        panel_vals = broadcast(column_vals, "col", panel % cols_n)
        gathered = jnp.stack(
            [broadcast(panel_vals, "row", my_col + r * cols_n) for r in range(ratio)]
        )
        col_vals = gathered.transpose(1, 0, 2, 3).reshape(blocks_c, width, width)
        product = jnp.einsum(
            "ian,jbn->iajb",
            panel_vals,
            col_vals,
            precision=lax.Precision.HIGHEST,
            preferred_element_type=jnp.float32,
        )
        mask_r = glob_r[:, None, None, None]
        mask_c = glob_c[None, None, :, None]
        fresh = jnp.where((mask_r > panel) & (mask_c > panel), current - product, current)
        fresh = jnp.where(mask_c == panel, panel_vals[:, :, None, :], fresh)
        current = jnp.where((mask_r == panel) & (mask_c > panel), 0.0, fresh)
    return current


def solution(mesh):
    in_specs = (P(None, "row", None, "col"),)
    out_specs = P(None, "row", None, "col")
    return jax.shard_map(shards, mesh=mesh, in_specs=in_specs, out_specs=out_specs, check_vma=False)
```

profile of v0, /device:TPU:1, one launch (start us, length us, event | category | flops | bytes accessed | tf_op | source)
XLA Modules:
  0.0 1427.4 jit_solution(3459192166164809112)
XLA Ops:
  8.6 139.3 %all-reduce.14.cloned.1.call-done = f32[256,256]{0,1:T(8,128)} async-done(((f32[256,256]{0,1:T(8,128)}), f32[256,256]{0,1:T(8,128)}) %all-reduce.14.cloned.1.call-update) | async-done | bytes 262160 | tf_op jit(solution)/shard_map/psum | solution.py:11
  149.1 11.7 cholesky.172
  160.9 9.8 custom-call.15
  171.2 11.7 cholesky.189
  185.0 4.2 while.6
  185.8 1.4 bitcast_dynamic-update-slice_fusion.6
  187.8 1.4 bitcast_dynamic-update-slice_fusion.6
  189.2 19.7 %custom-call.16 = f32[2,128,128]{1,2,0:T(8,128)S(1)} custom-call(f32[2,128,128]{2,1,0:T(8,128)S(1)} %get-tuple-element.27), custom_call_target="InvertDiagBlocksLowerTriangular" | custom-call | tf_op jit(solution)/shard_map/jit(_solve_triangular)/triangular_solve | solution.py:31
  210.8 126.2 %all-reduce.16.cloned.1.call-done = f32[1,256,256]{2,1,0:T(8,128)} async-done(((f32[1,256,256]{2,1,0:T(8,128)}), f32[1,256,256]{2,1,0:T(8,128)}) %all-reduce.16.cloned.1.call-update) | async-done | bytes 262160 | tf_op jit(solution)/shard_map/psum | solution.py:11
  337.0 1.8 select_bitcast_fusion.7
  339.9 140.8 %all-reduce.30.cloned.1.call-done = (f32[1,1,256,256]{3,2,1,0:T(8,128)}, f32[1,1,256,256]{3,2,1,0:T(8,128)}) async-done(((f32[1,1,256,256]{3,2,1,0:T(8,128)}, f32[1,1,256,256]{3,2,1,0:T(8,128)}), (f32[1,1,256,256]{3,2,1,0:T(8,128)}, f32[1,1,256,256]{3,2,1,0:T(8,128)})) %all-reduce.30.cloned.1.call-update) | async-done | bytes 524304 | tf_op jit(solution)/shard_map/psum | solution.py:11
  480.7 1.6 fusion.3
  483.2 132.6 %all-reduce.18.cloned.1.call-done = f32[256,256]{0,1:T(8,128)} async-done(((f32[256,256]{0,1:T(8,128)}), f32[256,256]{0,1:T(8,128)}) %all-reduce.18.cloned.1.call-update) | async-done | bytes 262160 | tf_op jit(solution)/shard_map/psum | solution.py:11
  617.0 11.7 cholesky.206
  628.8 9.8 custom-call.17
  639.1 11.7 cholesky.223
  653.5 4.2 while.7
  657.7 19.7 %custom-call.18 = f32[2,128,128]{1,2,0:T(8,128)S(1)} custom-call(f32[2,128,128]{2,1,0:T(8,128)S(1)} %get-tuple-element.28), custom_call_target="InvertDiagBlocksLowerTriangular" | custom-call | tf_op jit(solution)/shard_map/jit(_solve_triangular)/triangular_solve | solution.py:31
  679.3 126.3 %all-reduce.20.cloned.1.call-done = f32[1,256,256]{2,1,0:T(8,128)} async-done(((f32[1,256,256]{2,1,0:T(8,128)}), f32[1,256,256]{2,1,0:T(8,128)}) %all-reduce.20.cloned.1.call-update) | async-done | bytes 262160 | tf_op jit(solution)/shard_map/psum | solution.py:11
  805.5 1.8 select_bitcast_fusion.4
  808.4 141.0 %all-reduce.28.cloned.1.call-done = (f32[1,1,256,256]{3,2,1,0:T(8,128)}, f32[1,1,256,256]{3,2,1,0:T(8,128)}) async-done(((f32[1,1,256,256]{3,2,1,0:T(8,128)}, f32[1,1,256,256]{3,2,1,0:T(8,128)}), (f32[1,1,256,256]{3,2,1,0:T(8,128)}, f32[1,1,256,256]{3,2,1,0:T(8,128)})) %all-reduce.28.cloned.1.call-update) | async-done | bytes 524304 | tf_op jit(solution)/shard_map/psum | solution.py:11
  949.4 1.6 fusion.7
  951.8 132.5 %all-reduce.22.cloned.1.call-done = f32[256,256]{0,1:T(8,128)} async-done(((f32[256,256]{0,1:T(8,128)}), f32[256,256]{0,1:T(8,128)}) %all-reduce.22.cloned.1.call-update) | async-done | bytes 262160 | tf_op jit(solution)/shard_map/psum | solution.py:11
  1085.5 11.7 cholesky.240
  1097.3 9.8 custom-call.19
  1107.6 11.7 cholesky.257
  1122.0 4.2 while.8
  1126.2 19.7 %custom-call.20 = f32[2,128,128]{1,2,0:T(8,128)S(1)} custom-call(f32[2,128,128]{2,1,0:T(8,128)S(1)} %get-tuple-element.29), custom_call_target="InvertDiagBlocksLowerTriangular" | custom-call | tf_op jit(solution)/shard_map/jit(_solve_triangular)/triangular_solve | solution.py:31
  1147.8 126.3 %all-reduce.24.cloned.1.call-done = f32[1,256,256]{2,1,0:T(8,128)} async-done(((f32[1,256,256]{2,1,0:T(8,128)}), f32[1,256,256]{2,1,0:T(8,128)}) %all-reduce.24.cloned.1.call-update) | async-done | bytes 262160 | tf_op jit(solution)/shard_map/psum | solution.py:11
  1274.1 1.8 select_bitcast_fusion.1
  1277.0 140.8 %all-reduce.26.cloned.1.call-done = (f32[1,1,256,256]{3,2,1,0:T(8,128)}, f32[1,1,256,256]{3,2,1,0:T(8,128)}) async-done(((f32[1,1,256,256]{3,2,1,0:T(8,128)}, f32[1,1,256,256]{3,2,1,0:T(8,128)}), (f32[1,1,256,256]{3,2,1,0:T(8,128)}, f32[1,1,256,256]{3,2,1,0:T(8,128)})) %all-reduce.26.cloned.1.call-update) | async-done | bytes 524304 | tf_op jit(solution)/shard_map/psum | solution.py:11
  1417.8 1.6 fusion.11
  (112 shorter events, 31.1 us)
Async XLA Ops:
  6.5 141.4 %all-reduce.14.cloned.1.call-start = ((), (), s32[]{:S(2)}) async-start(), calls=%async_computation | async-start | bytes 524288 | tf_op jit(solution)/shard_map/psum | solution.py:11
  8.6 328.5 %all-reduce.16.cloned.1.call-start = ((), (), s32[]{:S(2)}) async-start(), calls=%async_computation.1 | async-start | bytes 524288 | tf_op jit(solution)/shard_map/psum | solution.py:11
  147.9 1.2 copy-start.3
  210.7 270.0 %all-reduce.30.cloned.1.call-start = ((), (), s32[]{:S(2)}) async-start(), calls=%async_computation.8 | async-start | bytes 1048576 | tf_op jit(solution)/shard_map/psum | solution.py:11
  338.8 0.9 copy-start
  338.8 277.0 %all-reduce.18.cloned.1.call-start = ((), (), s32[]{:S(2)}) async-start(), calls=%async_computation.2 | async-start | bytes 524288 | tf_op jit(solution)/shard_map/psum | solution.py:11
  483.1 322.4 %all-reduce.20.cloned.1.call-start = ((), (), s32[]{:S(2)}) async-start(), calls=%async_computation.3 | async-start | bytes 524288 | tf_op jit(solution)/shard_map/psum | solution.py:11
  615.8 1.2 copy-start.5
  679.2 270.2 %all-reduce.28.cloned.1.call-start = ((), (), s32[]{:S(2)}) async-start(), calls=%async_computation.7 | async-start | bytes 1048576 | tf_op jit(solution)/shard_map/psum | solution.py:11
  807.3 0.9 copy-start.1
  807.3 277.0 %all-reduce.22.cloned.1.call-start = ((), (), s32[]{:S(2)}) async-start(), calls=%async_computation.4 | async-start | bytes 524288 | tf_op jit(solution)/shard_map/psum | solution.py:11
  951.8 322.3 %all-reduce.24.cloned.1.call-start = ((), (), s32[]{:S(2)}) async-start(), calls=%async_computation.5 | async-start | bytes 524288 | tf_op jit(solution)/shard_map/psum | solution.py:11
  1084.3 1.2 copy-start.4
  1147.8 270.0 %all-reduce.26.cloned.1.call-start = ((), (), s32[]{:S(2)}) async-start(), calls=%async_computation.6 | async-start | bytes 1048576 | tf_op jit(solution)/shard_map/psum | solution.py:11
  1275.9 0.9 copy-start.2
Sparse Core Ops, SparseCore 0:
  10.6 137.2 all-reduce.13
  210.9 126.1 all-reduce.15
  340.2 140.4 all-reduce.29
  484.1 131.6 all-reduce.17
  679.3 126.1 all-reduce.19
  808.9 140.4 all-reduce.27
  952.6 131.6 all-reduce.21
  1147.9 126.1 all-reduce.23
  1277.3 140.4 all-reduce.25
where the time goes:
time: 1440 us; the launch traced here: 1430 us
  waiting for transfers between devices  1210 us (84%)
  other arithmetic  172 us (12%)
  local copies, waits for them, and re-layouts  20.9 us (1%)
  between operations  18 us (1%)
    psum x9, waiting for transfers between devices, broadcast(): return lax.psum(jnp.where(mine, array, jnp.zeros_like(array)), axis)  1210 us
    another operation x20, other arithmetic, shards(): factor = jnp.linalg.cholesky(corner)  103 us
    another operation x7, other arithmetic, shards(): solved = jax.scipy.linalg.solve_triangular(factor, stacked, lower=True)  59.1 us
  transfers between devices with their start and end apart: 9, of which 9 were waited for; matrix products, arithmetic and copies ran while one was open for 0% of the time, Pallas kernels for 0%

commit v1 on v0

v1 whole, which is shorter than its diff:
```python
import jax
import jax.numpy as jnp
from jax import lax
from jax.experimental import pallas as pl
from jax.experimental.pallas import tpu as pltpu
from jax.sharding import PartitionSpec as P

PANELS = 3
W = 128
NB = 256
N = PANELS * NB
UPPER = [(r, c) for r in range(PANELS) for c in range(r, PANELS)]


def dot(a, b, ca=1, cb=0):
    return lax.dot_general(
        a,
        b,
        (((ca,), (cb,)), ((), ())),
        precision=lax.Precision.HIGHEST,
        preferred_element_type=jnp.float32,
    )


def lane_of(x, k):
    return jnp.broadcast_to(x[:, k : k + 1], (8, W))


def row_of(x, s):
    return jnp.broadcast_to(x[s : s + 1, :], (8, W))


def factor(block):
    groups = W // 8
    lane = lax.broadcasted_iota(jnp.int32, (8, W), 1)
    sub = lax.broadcasted_iota(jnp.int32, (8, W), 0)
    x = [block[8 * p : 8 * p + 8, :] for p in range(groups)]
    v = [jnp.where(lane == sub + 8 * p, 1.0, 0.0).astype(jnp.float32) for p in range(groups)]
    upper, inverse = [], []
    for p in range(groups):
        k = 8 * p
        cols = [lane_of(x[p], k + j) for j in range(8)]
        e = [[row_of(cols[j], s) if s >= j else None for j in range(8)] for s in range(8)]
        r = [row_of(x[p], j) for j in range(8)]
        z = [row_of(v[p], j) for j in range(8)]
        low = [[None] * 8 for _ in range(8)]
        inv = [None] * 8
        for j in range(8):
            inv[j] = 1.0 / e[j][j]
            for s in range(j + 1, 8):
                low[s][j] = e[s][j] * inv[j]
            for s in range(j + 1, 8):
                for t in range(j + 1, s + 1):
                    e[s][t] = e[s][t] - low[s][j] * e[t][j]
                r[s] = r[s] - low[s][j] * r[j]
                z[s] = z[s] - low[s][j] * z[j]
        sr = [r[j] * inv[j] for j in range(8)]
        sz = [z[j] * inv[j] for j in range(8)]
        for q in range(p + 1, groups):
            c = [lane_of(x[q], k + j) for j in range(8)]
            for j in range(8):
                for s in range(j + 1, 8):
                    c[s] = c[s] - low[s][j] * c[j]
            ax, av = c[0] * sr[0], c[0] * sz[0]
            for j in range(1, 8):
                ax, av = ax + c[j] * sr[j], av + c[j] * sz[j]
            x[q], v[q] = x[q] - ax, v[q] - av
        root = lax.rsqrt(e[0][0])
        u, w = r[0] * root, z[0] * root
        for j in range(1, 8):
            root = lax.rsqrt(e[j][j])
            u, w = jnp.where(sub == j, r[j] * root, u), jnp.where(sub == j, z[j] * root, w)
        upper.append(jnp.where(lane >= sub + k, u, 0.0))
        inverse.append(w)
    return jnp.concatenate(upper, 0), jnp.concatenate(inverse, 0)


def lead_kernel(a_ref, u_ref, v_ref, s_ref):
    s_ref[...] = jnp.zeros_like(s_ref)
    for n, (r, c) in enumerate(UPPER):
        s_ref[NB * r : NB * r + NB, NB * c : NB * c + NB] = a_ref[:, n, :, :].reshape(NB, NB)
    u_ref[...] = jnp.zeros_like(u_ref)
    v_ref[...] = jnp.zeros_like(v_ref)

    def body(b, carry):
        o = pl.multiple_of(b * W, W)
        upper, inverse = factor(s_ref[pl.ds(o, W), pl.ds(o, W)])
        v_ref[pl.ds(o, W), pl.ds(pl.multiple_of((b % 2) * W, W), W)] = inverse
        rest = dot(inverse, s_ref[pl.ds(o, W), :])
        lane = lax.broadcasted_iota(jnp.int32, rest.shape, 1)
        rest = jnp.where(lane >= o + W, rest, 0.0)
        u_ref[pl.ds(o, W), :] = rest
        u_ref[pl.ds(o, W), pl.ds(o, W)] = upper
        s_ref[...] = s_ref[...] - dot(rest, rest, 0, 0)
        return carry

    lax.fori_loop(0, N // W, body, 0)
    for k in range(PANELS):
        o, m = NB * k, NB * k + W
        cross = dot(u_ref[o : o + W, m : m + W], v_ref[o : o + W, 0:W], 0, 0)
        v_ref[m : m + W, 0:W] = -dot(v_ref[m : m + W, W:NB], cross)


def update_kernel(place_ref, t_ref, p_ref, u_ref, v_ref, m_ref, o_ref, w_ref, y_ref):
    i, c = place_ref[0], place_ref[1]
    for k in range(PANELS):
        o = NB * k
        t = t_ref[:, k, :, :].reshape(NB, 2 * NB)
        y = p_ref[k]
        if k:
            t = t - dot(u_ref[0:o, o : o + NB], w_ref[0:o, :], 0, 0)
            y = y - dot(y_ref[:, 0:o], u_ref[0:o, o : o + NB])
        w_ref[o : o + NB, :] = dot(v_ref[o : o + NB, :], t)
        y_ref[:, o : o + NB] = dot(y, v_ref[o : o + NB, :], 1, 1)

    @pl.when(i < PANELS)
    def _():
        y_ref[...] = u_ref[:, pl.ds(pl.multiple_of(jnp.minimum(i, PANELS - 1) * NB, NB), NB)].T

    product = dot(y_ref[...], w_ref[...])
    keep = i >= PANELS
    o_ref[1] = jnp.where(keep, m_ref[1] - product[:, NB:], 0.0)

    @pl.when(c >= PANELS)
    def _():
        o_ref[0] = jnp.where(keep, m_ref[0] - product[:, :NB], 0.0)

    @pl.when(c < PANELS)
    def _():
        o_ref[0] = y_ref[:, pl.ds(pl.multiple_of(jnp.minimum(c, PANELS - 1) * NB, NB), NB)]


def shards(matrix):
    rows_n = lax.axis_size("row")
    my_row = lax.axis_index("row")
    my_col = lax.axis_index("col")
    step = NB // rows_n
    mine = matrix[0].transpose(1, 0, 2)
    panel = lax.all_gather(mine[0], "col")[:PANELS]
    pieces = mine.reshape(2, rows_n, step, NB).transpose(1, 0, 2, 3)
    pieces = lax.all_to_all(pieces, "row", 0, 0)[:PANELS]
    top = jnp.concatenate([pieces[:, 0], pieces[:, 1]], -1)
    tops = lax.all_gather(top, "row")
    heads = lax.all_gather(pieces[:, 0], "col")
    head = jnp.stack([heads[c, r] for r, c in UPPER])
    lead = lax.all_to_all(jnp.broadcast_to(head[None], (rows_n,) + head.shape), "row", 0, 0)
    f32 = jnp.float32
    upper, inverse = pl.pallas_call(
        lead_kernel,
        out_shape=[jax.ShapeDtypeStruct((N, N), f32), jax.ShapeDtypeStruct((N, NB), f32)],
        scratch_shapes=[pltpu.VMEM((N, N), f32)],
        compiler_params=pltpu.CompilerParams(vmem_limit_bytes=32 << 20),
        cost_estimate=pl.CostEstimate(flops=2 << 30, bytes_accessed=8 << 20, transcendentals=0),
    )(lead)
    place = jnp.stack([my_row, my_col]).astype(jnp.int32)
    vmem = pl.BlockSpec(memory_space=pltpu.VMEM)
    out = pl.pallas_call(
        update_kernel,
        out_shape=jax.ShapeDtypeStruct((2, NB, NB), f32),
        in_specs=[pl.BlockSpec(memory_space=pltpu.SMEM)] + [vmem] * 5,
        out_specs=vmem,
        scratch_shapes=[pltpu.VMEM((N, 2 * NB), f32), pltpu.VMEM((NB, N), f32)],
        compiler_params=pltpu.CompilerParams(vmem_limit_bytes=32 << 20),
        cost_estimate=pl.CostEstimate(flops=2 << 30, bytes_accessed=8 << 20, transcendentals=0),
    )(place, tops, panel, upper, inverse, mine)
    return out.transpose(1, 0, 2)[None]


def solution(mesh):
    spec = P(None, "row", None, "col")
    return jax.shard_map(shards, mesh=mesh, in_specs=(spec,), out_specs=spec, check_vma=False)
```

time: 1440 us -> 171 us (0.12)
  waiting for transfers between devices: 1210 us -> 30.2 us
  other arithmetic: 172 us -> 0.7 us
  blocking collectives: 0 us -> 55.1 us
  Pallas kernels: 0 us -> 52.8 us
    psum x9 -> x0, waiting for transfers between devices: 1210 us -> none  [broadcast(): return lax.psum(jnp.where(mine, array, jnp.zeros_like(array)), axis)]
    another operation x30 -> x1, other arithmetic: 168 us -> 0.08 us  [shards(): place = jnp.stack([my_row, my_col]).astype(jnp.int32)]
    pallas_call x0 -> x2, Pallas kernels: none -> 52.8 us  [the longest x1 46.2 us: shards(): pl.pallas_call(lead_kernel, out_shape=[jax.ShapeDtypeStruct((N, N), f32),...]
    all_gather x0 -> x1, blocking collectives: none -> 33.8 us  [shards(): heads = lax.all_gather(pieces[:, 0], 'col')]
    all_to_all x0 -> x1, waiting for transfers between devices: none -> 22.7 us  [shards(): lax.all_to_all(jnp.broadcast_to(head[None], (rows_n,) + head.shape), 'row...]
    all_to_all x0 -> x1, blocking collectives: none -> 21.3 us  [shards(): pieces = lax.all_to_all(pieces, 'row', 0, 0)[:PANELS]]
  transfers between devices with their start and end apart: 9 -> 3, of which waited for: 9 -> 2; matrix products, arithmetic and copies ran while one was open for 0% -> 2% of each run, Pallas kernels for 0% -> 27%
where the time goes in v1:
time: 171 us
  blocking collectives  55.1 us (32%)
  Pallas kernels  52.8 us (31%)
  waiting for transfers between devices  30.2 us (18%)
  between operations  13.5 us (8%)
  local copies, waits for them, and re-layouts  10.1 us (6%)
  starting transfers between devices  8.25 us (5%)
    pallas_call x1, Pallas kernels, shards(): pl.pallas_call(lead_kernel, out_shape=[jax.ShapeDtypeStruct((N, N), f32),...  46.2 us
    all_gather x1, blocking collectives, shards(): heads = lax.all_gather(pieces[:, 0], 'col')  33.8 us
    all_to_all x1, waiting for transfers between devices, shards(): lax.all_to_all(jnp.broadcast_to(head[None], (rows_n,) + head.shape), 'row...  22.7 us
    all_to_all x1, blocking collectives, shards(): pieces = lax.all_to_all(pieces, 'row', 0, 0)[:PANELS]  21.3 us
    all_to_all x1, starting transfers between devices, shards(): lax.all_to_all(jnp.broadcast_to(head[None], (rows_n,) + head.shape), 'row...  8.2 us
    all_gather x1, waiting for transfers between devices, shards(): tops = lax.all_gather(top, 'row')  7.49 us
    pallas_call x1, Pallas kernels, shards(): pl.pallas_call(update_kernel, out_shape=jax.ShapeDtypeStruct((2, NB, NB),...  6.59 us
    unnamed x12, local copies, waits for them, and re-layouts  5.58 us
  transfers between devices with their start and end apart: 3, of which 2 were waited for; matrix products, arithmetic and copies ran while one was open for 2% of the time, Pallas kernels for 27%

profile of v1, /device:TPU:1, one launch (start us, length us, event | category | flops | bytes accessed | tf_op | source)
XLA Modules:
  0.0 170.6 jit_solution(13328235990489538973)
XLA Ops:
  6.5 0.0 all-gather.5.cloned.1.call-start
  6.5 1.1 copy.14
  7.6 0.7 slice.46
  8.3 0.0 all-gather.5.cloned.1.call-update
  8.4 0.0 all-gather.7.cloned.1.call-start
  8.4 0.1 copy.13
  8.5 21.3 %all_to_all.10 = f32[32,2,8,256]{3,2,1,0:T(8,128)S(1)} all-to-all(f32[32,2,8,256]{3,2,1,0:T(8,128)S(1)} %bitcast.55), channel_id=1, replica_groups=mesh['row'=32,'col'=16] {'row'}, dimensions={0} | all-to-all | bytes 1048576 | tf_op jit(solution)/shard_map/all_to_all | solution.py:141
  29.7 0.6 pad_maximum_fusion
  30.4 33.8 %all-gather.1 = f32[48,1,8,256]{3,2,1,0:T(8,128)S(1)} all-gather(f32[3,1,8,256]{3,2,1,0:T(8,128)S(1)} %get-tuple-element.9), channel_id=3, replica_groups=mesh['row'=32,'col'=16] {'col'}, dimensions={0}, use_global_device_ids=true | all-gather | bytes 417792 | tf_op jit(solution)/shard_map/all_gather | solution.py:144
  64.2 0.0 all-gather.7.cloned.1.call-update
  64.2 1.3 broadcast_in_dim.4
  65.6 8.2 %all-to-all-start.1 = ((f32[32,6,8,256]{3,2,1,0:T(8,128)}), f32[32,6,8,256]{3,2,1,0:T(8,128)S(1)}, u32[]{:S(2)}, u32[]{:S(2)}) async-start(f32[32,6,8,256]{3,2,1,0:T(8,128)} %broadcast_in_dim.4), calls=%async_computation.1 | async-start | bytes 3145728 | tf_op jit(solution)/shard_map/all_to_all | solution.py:146
  73.8 0.1 pad_add_fusion.place_ref
  73.9 22.7 %all-to-all-done.1.a_ref = f32[32,6,8,256]{3,2,1,0:T(8,128)S(1)} async-done(((f32[32,6,8,256]{3,2,1,0:T(8,128)}), f32[32,6,8,256]{3,2,1,0:T(8,128)S(1)}, u32[]{:S(2)}, u32[]{:S(2)}) %all-to-all-start.1) | async-done | bytes 1572896 | tf_op jit(solution)/shard_map/all_to_all | solution.py:146
  96.6 46.2 %shard_map.17 = (f32[768,768]{1,0:T(8,128)S(1)}, f32[768,256]{1,0:T(8,128)S(1)}) custom-call(f32[32,6,8,256]{3,2,1,0:T(8,128)S(1)} %all-to-all-done.1.a_ref), custom_call_target="tpu_custom_call" | custom-call | flops 2147483648 | bytes 8388608 | tf_op jit(solution)/shard_map/pallas_call | solution.py:148
  142.8 0.0 copy-start.1
  142.8 1.4 copy-done.1
  144.2 0.0 all-gather.5.cloned.1.call-done
  144.2 1.2 slice.47.p_ref
  145.4 7.5 %all-gather.7.cloned.1.call-done = f32[96,8,512]{2,1,0:T(8,128)} async-done(((f32[3,8,512]{2,1,0:T(8,128)}), f32[96,8,512]{2,1,0:T(8,128)}) %all-gather.7.cloned.1.call-update) | async-done | bytes 1572880 | tf_op jit(solution)/shard_map/all_gather | solution.py:143
  152.9 0.0 copy-start
  152.9 1.4 copy-done
  154.3 0.0 copy-start.2
  154.3 1.7 copy-done.2
  156.0 6.6 %shard_map.18 = f32[2,256,256]{2,1,0:T(8,128)S(1)} custom-call(s32[2]{0:T(128)S(1)} %pad_add_fusion.place_ref, f32[32,3,8,512]{3,2,1,0:T(8,128)S(1)} %bitcast.54, f32[3,256,256]{2,1,0:T(8,128)S(1)} %slice.47.p_ref, f32[768,768]{1,0:T(8,128)S(1)} %copy-done.2, f32[768,256]{1,0:T(8,128)S(1)} %get-tuple-element.8.v_ref, f32[2,256,256]{2,1,0:T(8,128)S(1)} %bitcast.52), custom_call_target="tpu_custom_call" | custom-call | flops 2147483648 | bytes 8388608 | tf_op jit(solution)/shard_map/pallas_call | solution.py:157
  162.6 1.2 copy.8
  (7 shorter events, 0.0 us)
Async XLA Ops:
  6.5 137.7 %all-gather.5.cloned.1.call-start = ((), (), s32[]{:S(2)}) async-start(), calls=%async_computation.2 | async-start | bytes 4456448 | tf_op jit(solution)/shard_map/all_gather | solution.py:139
  8.4 144.5 %all-gather.7.cloned.1.call-start = ((), (), s32[]{:S(2)}) async-start(), calls=%async_computation.3 | async-start | bytes 1622016 | tf_op jit(solution)/shard_map/all_gather | solution.py:143
  65.6 31.0 %all-to-all-start.1 = ((f32[32,6,8,256]{3,2,1,0:T(8,128)}), f32[32,6,8,256]{3,2,1,0:T(8,128)S(1)}, u32[]{:S(2)}, u32[]{:S(2)}) async-start(f32[32,6,8,256]{3,2,1,0:T(8,128)} %broadcast_in_dim.4), calls=%async_computation.1 | async-start | bytes 3145728 | tf_op jit(solution)/shard_map/all_to_all | solution.py:146
  142.8 1.4 copy-start.1
  152.9 1.4 copy-start
  154.3 1.7 copy-start.2
Sparse Core Ops, SparseCore 0:
  9.4 77.4 all-gather.4
  90.1 62.7 all-gather.6

commit v2 on v1

v2 whole, which is shorter than its diff:
```python
import jax
import jax.numpy as jnp
from jax import lax
from jax.experimental import pallas as pl
from jax.experimental.pallas import tpu as pltpu
from jax.sharding import PartitionSpec as P

PANELS = 3
W = 128
NB = 256
N = PANELS * NB
UPPER = [(r, c) for c in range(PANELS) for r in range(c + 1)]


def dot(a, b, ca=1, cb=0):
    return lax.dot_general(
        a,
        b,
        (((ca,), (cb,)), ((), ())),
        precision=lax.Precision.HIGHEST,
        preferred_element_type=jnp.float32,
    )


def lane_of(x, k):
    return jnp.broadcast_to(x[:, k : k + 1], (8, W))


def row_of(x, s):
    return jnp.broadcast_to(x[s : s + 1, :], (8, W))


def factor(block):
    groups = W // 8
    lane = lax.broadcasted_iota(jnp.int32, (8, W), 1)
    sub = lax.broadcasted_iota(jnp.int32, (8, W), 0)
    x = [block[8 * p : 8 * p + 8, :] for p in range(groups)]
    v = [jnp.where(lane == sub + 8 * p, 1.0, 0.0).astype(jnp.float32) for p in range(groups)]
    upper, inverse = [], []
    d = [lane_of(x[0], t) for t in range(8)]
    for p in range(groups):
        k = 8 * p
        later = range(p + 1, groups)
        c = {q: [lane_of(x[q], k + j) for j in range(8)] for q in later}
        ahead = [lane_of(x[p + 1], k + 8 + t) for t in range(8)] if later else None
        r = [row_of(x[p], j) for j in range(8)]
        z = [row_of(v[p], j) for j in range(8)]
        inv, root = [None] * 8, None
        for j in range(8):
            pivot = row_of(d[j], j)
            inv[j] = 1.0 / pivot
            root = lax.rsqrt(pivot) if j == 0 else jnp.where(sub == j, lax.rsqrt(pivot), root)
            for s in range(j + 1, 8):
                low = row_of(d[j], s) * inv[j]
                d[s] = d[s] - d[j] * low
                r[s] = r[s] - low * r[j]
                z[s] = z[s] - low * z[j]
                for q in later:
                    c[q][s] = c[q][s] - low * c[q][j]
        if later:
            for j in range(8):
                scaled = c[p + 1][j] * inv[j]
                for t in range(8):
                    ahead[t] = ahead[t] - c[p + 1][j] * row_of(scaled, t)
        sr = [r[j] * inv[j] for j in range(8)]
        sz = [z[j] * inv[j] for j in range(8)]
        for q in later:
            ax, av = c[q][0] * sr[0], c[q][0] * sz[0]
            for j in range(1, 8):
                ax, av = ax + c[q][j] * sr[j], av + c[q][j] * sz[j]
            x[q], v[q] = x[q] - ax, v[q] - av
        u, w = r[0], z[0]
        for j in range(1, 8):
            u, w = jnp.where(sub == j, r[j], u), jnp.where(sub == j, z[j], w)
        upper.append(jnp.where(lane >= sub + k, u * root, 0.0))
        inverse.append(w * root)
        d = ahead
    return jnp.concatenate(upper, 0), jnp.concatenate(inverse, 0)


def lead_kernel(source_ref, u_ref, v_ref, a_ref, s_ref, d_ref, row_ref, last_ref, sem):
    arrival = pltpu.make_async_copy(source_ref, a_ref, sem)
    arrival.start()
    u_ref[...] = jnp.zeros_like(u_ref)
    v_ref[...] = jnp.zeros_like(v_ref)
    arrival.wait()
    for n, (r, c) in enumerate(UPPER):
        s_ref[NB * r : NB * r + NB, NB * c : NB * c + NB] = a_ref[:, n, :, :].reshape(NB, NB)
    for r in range(1, PANELS):
        s_ref[NB * r : NB * r + NB, 0 : NB * r] = jnp.zeros((NB, NB * r), jnp.float32)
    row_ref[...] = jnp.zeros_like(row_ref)
    last_ref[...] = jnp.zeros_like(last_ref)
    d_ref[...] = s_ref[0:W, 0:W]
    lane = lax.broadcasted_iota(jnp.int32, (W, N), 1)

    def body(b, carry):
        o = pl.multiple_of(b * W, W)
        before = pl.multiple_of(jnp.maximum(b - 1, 0) * W, W)
        after = pl.multiple_of(jnp.minimum(b + 1, N // W - 1) * W, W)
        rest = dot(last_ref[...], row_ref[...])
        u_ref[pl.ds(before, W), :] = jnp.where(lane >= o, rest, u_ref[pl.ds(before, W), :])
        row_ref[...] = s_ref[pl.ds(o, W), :] - dot(u_ref[:, pl.ds(o, W)], u_ref[...], 0, 0)
        ahead = u_ref[:, pl.ds(after, W)]
        corner = s_ref[pl.ds(after, W), pl.ds(after, W)] - dot(ahead, ahead, 0, 0)
        upper, inverse = factor(d_ref[...])
        u_ref[pl.ds(o, W), pl.ds(o, W)] = upper
        v_ref[pl.ds(o, W), pl.ds(pl.multiple_of((b % 2) * W, W), W)] = inverse
        last_ref[...] = inverse
        beside = dot(inverse, row_ref[:, pl.ds(after, W)])
        d_ref[...] = corner - dot(beside, beside, 0, 0)
        return carry

    lax.fori_loop(0, N // W, body, 0)
    for k in range(PANELS):
        o, m = NB * k, NB * k + W
        cross = dot(u_ref[o : o + W, m : m + W], v_ref[o : o + W, 0:W], 0, 0)
        v_ref[m : m + W, 0:W] = -dot(v_ref[m : m + W, W:NB], cross)


def update_kernel(place_ref, tops_ref, panel_ref, u_ref, v_ref, m_ref, o_ref, t_ref, p_ref, w_ref, y_ref, sems):
    i, c = place_ref[0], place_ref[1]
    arrivals = []
    for k in range(PANELS):
        arrivals.append(pltpu.make_async_copy(tops_ref.at[:, k], t_ref.at[:, k], sems.at[0, k]))
        arrivals.append(pltpu.make_async_copy(panel_ref.at[k], p_ref.at[k], sems.at[1, k]))
    for arrival in arrivals:
        arrival.start()
    for k in range(PANELS):
        o = NB * k
        arrivals[2 * k].wait()
        arrivals[2 * k + 1].wait()
        t = jnp.concatenate([t_ref[:, k, n, :, :].reshape(NB, NB) for n in range(2)], 1)
        y = p_ref[k]
        if k:
            t = t - dot(u_ref[0:o, o : o + NB], w_ref[0:o, :], 0, 0)
            y = y - dot(y_ref[:, 0:o], u_ref[0:o, o : o + NB])
        w_ref[o : o + NB, :] = dot(v_ref[o : o + NB, :], t)
        y_ref[:, o : o + NB] = dot(y, v_ref[o : o + NB, :], 1, 1)

    @pl.when(i < PANELS)
    def _():
        y_ref[...] = u_ref[:, pl.ds(pl.multiple_of(jnp.minimum(i, PANELS - 1) * NB, NB), NB)].T

    product = dot(y_ref[...], w_ref[...])
    keep = i >= PANELS
    o_ref[1] = jnp.where(keep, m_ref[1] - product[:, NB:], 0.0)

    @pl.when(c >= PANELS)
    def _():
        o_ref[0] = jnp.where(keep, m_ref[0] - product[:, :NB], 0.0)

    @pl.when(c < PANELS)
    def _():
        o_ref[0] = y_ref[:, pl.ds(pl.multiple_of(jnp.minimum(c, PANELS - 1) * NB, NB), NB)]


def copies(array, count):
    return jnp.broadcast_to(array[None], (count,) + array.shape)


def shards(matrix):
    rows_n = lax.axis_size("row")
    my_row = lax.axis_index("row")
    my_col = lax.axis_index("col")
    step = NB // rows_n
    cols_n = lax.axis_size("col")
    mine = matrix[0].transpose(1, 0, 2)
    pieces = mine.reshape(2, rows_n, step, NB).transpose(1, 0, 2, 3)
    pieces = lax.all_to_all(pieces, "row", 0, 0)[:PANELS]
    heads = lax.all_to_all(copies(pieces[:, 0], cols_n), "col", 0, 0)
    head = jnp.concatenate([heads[c, : c + 1] for c in range(PANELS)])
    lead = lax.all_to_all(copies(head, rows_n), "row", 0, 0)
    lead, pieces = lax.optimization_barrier((lead, pieces))
    tops = lax.all_to_all(copies(pieces, rows_n), "row", 0, 0)
    panel = lax.all_gather(mine[0], "col")
    f32 = jnp.float32
    hbm = pl.BlockSpec(memory_space=pltpu.HBM)
    upper, inverse = pl.pallas_call(
        lead_kernel,
        out_shape=[jax.ShapeDtypeStruct((N, N), f32), jax.ShapeDtypeStruct((N, NB), f32)],
        in_specs=[hbm],
        scratch_shapes=[
            pltpu.VMEM(lead.shape, f32),
            pltpu.VMEM((N, N), f32),
            pltpu.VMEM((W, W), f32),
            pltpu.VMEM((W, N), f32),
            pltpu.VMEM((W, W), f32),
            pltpu.SemaphoreType.DMA,
        ],
        compiler_params=pltpu.CompilerParams(vmem_limit_bytes=56 << 20),
        cost_estimate=pl.CostEstimate(flops=2 << 30, bytes_accessed=100 << 20, transcendentals=0),
    )(lead)
    place = jnp.stack([my_row, my_col]).astype(jnp.int32)
    vmem = pl.BlockSpec(memory_space=pltpu.VMEM)
    out = pl.pallas_call(
        update_kernel,
        out_shape=jax.ShapeDtypeStruct((2, NB, NB), f32),
        in_specs=[pl.BlockSpec(memory_space=pltpu.SMEM), hbm, hbm, vmem, vmem, vmem],
        out_specs=vmem,
        scratch_shapes=[
            pltpu.VMEM(tops.shape, f32),
            pltpu.VMEM((PANELS, NB, NB), f32),
            pltpu.VMEM((N, 2 * NB), f32),
            pltpu.VMEM((NB, N), f32),
            pltpu.SemaphoreType.DMA((2, PANELS)),
        ],
        compiler_params=pltpu.CompilerParams(vmem_limit_bytes=56 << 20),
        cost_estimate=pl.CostEstimate(flops=2 << 30, bytes_accessed=8 << 20, transcendentals=0),
    )(place, tops, panel, upper, inverse, mine)
    return out.transpose(1, 0, 2)[None]


def solution(mesh):
    spec = P(None, "row", None, "col")
    return jax.shard_map(shards, mesh=mesh, in_specs=(spec,), out_specs=spec, check_vma=False)
```

time: 171 us -> 161 us (0.942)
  Pallas kernels: 52.8 us -> 44.1 us
  waiting for transfers between devices: 30.2 us -> 22.7 us
  blocking collectives: 55.1 us -> 61.2 us
  starting transfers between devices: 8.25 us -> 10.1 us
  local copies, waits for them, and re-layouts: 10.1 us -> 8.34 us
    all_to_all x0 -> x1, blocking collectives: none -> 39.9 us  [shards(): heads = lax.all_to_all(copies(pieces[:, 0], cols_n), 'col', 0, 0)]
    all_gather x1 -> x0, blocking collectives: 33.8 us -> none  [shards(): heads = lax.all_gather(pieces[:, 0], 'col')]
    pallas_call x1, Pallas kernels: 46.2 us -> 33.2 us  [shards(): pl.pallas_call(lead_kernel, out_shape=[jax.ShapeDtypeStruct((N, N), f32),...]
    all_gather x2 -> x1, waiting for transfers between devices: 7.49 us -> 0.02 us  [shards(): panel = lax.all_gather(mine[0], 'col')]
    pallas_call x1, Pallas kernels: 6.59 us -> 10.8 us  [shards(): pl.pallas_call(update_kernel, out_shape=jax.ShapeDtypeStruct((2, NB, NB),...]
    unnamed x12 -> x7, local copies, waits for them, and re-layouts: 5.58 us -> 2.37 us
    all_to_all x1 -> x2, starting transfers between devices: 8.2 us -> 10.1 us  [the longest x1 5.76 us: shards(): lead = lax.all_to_all(copies(head, rows_n), 'row', 0, 0)]
    all_to_all x1 -> x2, waiting for transfers between devices: 22.7 us -> 22.7 us  [the longest x1 22.7 us: shards(): lead = lax.all_to_all(copies(head, rows_n), 'row', 0, 0)]
  transfers between devices with their start and end apart: 3 -> 3, of which waited for: 2 -> 1; matrix products, arithmetic and copies ran while one was open for 2% -> 2% of each run, Pallas kernels for 27% -> 21%
where the time goes in v2:
time: 161 us
  blocking collectives  61.2 us (38%)
  Pallas kernels  44.1 us (27%)
  waiting for transfers between devices  22.7 us (14%)
  between operations  13.5 us (8%)
  starting transfers between devices  10.1 us (6%)
  local copies, waits for them, and re-layouts  8.34 us (5%)
    all_to_all x1, blocking collectives, shards(): heads = lax.all_to_all(copies(pieces[:, 0], cols_n), 'col', 0, 0)  39.9 us
    pallas_call x1, Pallas kernels, shards(): pl.pallas_call(lead_kernel, out_shape=[jax.ShapeDtypeStruct((N, N), f32),...  33.2 us
    all_to_all x1, waiting for transfers between devices, shards(): lead = lax.all_to_all(copies(head, rows_n), 'row', 0, 0)  22.7 us
    all_to_all x1, blocking collectives, shards(): pieces = lax.all_to_all(pieces, 'row', 0, 0)[:PANELS]  21.3 us
    pallas_call x1, Pallas kernels, shards(): pl.pallas_call(update_kernel, out_shape=jax.ShapeDtypeStruct((2, NB, NB),...  10.8 us
    all_to_all x1, starting transfers between devices, shards(): lead = lax.all_to_all(copies(head, rows_n), 'row', 0, 0)  5.76 us
    all_to_all x1, starting transfers between devices, shards(): tops = lax.all_to_all(copies(pieces, rows_n), 'row', 0, 0)  4.31 us
  transfers between devices with their start and end apart: 3, of which 1 were waited for; matrix products, arithmetic and copies ran while one was open for 2% of the time, Pallas kernels for 21%

profile of v2, /device:TPU:1, one launch (start us, length us, event | category | flops | bytes accessed | tf_op | source)
XLA Modules:
  0.0 160.6 jit_solution(14962971023582194313)
XLA Ops:
  6.5 0.0 all-gather.2.cloned.1.call-start
  6.5 1.1 copy.12
  7.6 0.0 copy-start
  7.6 0.8 slice.30
  8.4 0.0 all-gather.2.cloned.1.call-update
  8.4 0.1 copy.11
  8.5 21.3 %all_to_all.20 = f32[32,2,8,256]{3,2,1,0:T(8,128)S(1)} all-to-all(f32[32,2,8,256]{3,2,1,0:T(8,128)S(1)} %bitcast.28), channel_id=1, replica_groups=mesh['row'=32,'col'=16] {'row'}, dimensions={0} | all-to-all | bytes 1048576 | tf_op jit(solution)/shard_map/all_to_all | solution.py:169
  29.8 0.0 copy-done
  29.8 39.9 %all_to_all.21 = f32[16,3,8,256]{3,2,1,0:T(8,128)S(1)} all-to-all(f32[16,3,8,256]{3,2,1,0:T(8,128)S(1)} %broadcast_in_dim.11), channel_id=1, replica_groups=mesh['row'=32,'col'=16] {'col'}, dimensions={0} | all-to-all | bytes 786432 | tf_op jit(solution)/shard_map/all_to_all | solution.py:170
  69.8 1.4 broadcast_in_dim.24
  71.1 5.8 %all-to-all-start.2 = ((f32[32,6,8,256]{3,2,1,0:T(8,128)}), f32[32,6,8,256]{3,2,1,0:T(8,128)S(1)}, u32[]{:S(2)}, u32[]{:S(2)}) async-start(f32[32,6,8,256]{3,2,1,0:T(8,128)} %broadcast_in_dim.24), calls=%async_computation.2 | async-start | bytes 3145728 | tf_op jit(solution)/shard_map/all_to_all | solution.py:172
  76.9 22.7 %all-to-all-done.2.source_ref = f32[32,6,8,256]{3,2,1,0:T(8,128)S(1)} async-done(((f32[32,6,8,256]{3,2,1,0:T(8,128)}), f32[32,6,8,256]{3,2,1,0:T(8,128)S(1)}, u32[]{:S(2)}, u32[]{:S(2)}) %all-to-all-start.2) | async-done | bytes 1572896 | tf_op jit(solution)/shard_map/all_to_all | solution.py:172
  99.6 0.0 copy-start.2
  99.6 1.5 broadcast_in_dim.25
  101.1 0.2 copy-done.2
  101.3 4.3 %all-to-all-start.3 = ((f32[32,3,2,8,256]{4,3,2,1,0:T(8,128)}), f32[32,3,2,8,256]{4,3,2,1,0:T(8,128)S(1)}, u32[]{:S(2)}, u32[]{:S(2)}) async-start(f32[32,3,2,8,256]{4,3,2,1,0:T(8,128)} %broadcast_in_dim.25), calls=%async_computation.3 | async-start | bytes 3145728 | tf_op jit(solution)/shard_map/all_to_all | solution.py:174
  105.6 0.7 pad_add_fusion.place_ref
  106.2 33.2 %shard_map.17 = (f32[768,768]{1,0:T(8,128)}, f32[768,256]{1,0:T(8,128)}) custom-call(f32[32,6,8,256]{3,2,1,0:T(8,128)} %copy-done.2), custom_call_target="tpu_custom_call" | custom-call | flops 2147483648 | bytes 104857600 | tf_op jit(solution)/shard_map/pallas_call | solution.py:178
  139.5 0.0 all-to-all-done.3.tops_ref
  139.5 0.0 copy-start.1
  139.5 0.0 all-gather.2.cloned.1.call-done.panel_ref
  139.5 1.1 copy-done.1
  140.6 10.8 %shard_map.18 = f32[2,256,256]{2,1,0:T(8,128)} custom-call(s32[2]{0:T(128)} %pad_add_fusion.place_ref, f32[32,3,2,8,256]{4,3,2,1,0:T(8,128)} %copy-done.1, f32[16,256,256]{2,1,0:T(8,128)} %all-gather.2.cloned.1.call-done.panel_ref, f32[768,768]{1,0:T(8,128)} %get-tuple-element.11.u_ref, f32[768,256]{1,0:T(8,128)} %get-tuple-element.12.v_ref, ...), custom_call_target="tpu_custom_call" | custom-call | flops 2147483648 | bytes 8388608 | tf_op jit(solution)/shard_map/pallas_call | solution.py:195
  151.5 2.2 %copy.7 = f32[1,256,2,256]{3,2,1,0:T(2,128)} copy(f32[1,256,2,256]{3,1,2,0:T(8,128)} %bitcast.27) | data formatting | bytes 1048576 | tf_op jit(solution)/shard_map/broadcast_in_dim | solution.py:210
  (7 shorter events, 0.1 us)
Async XLA Ops:
  6.5 133.0 %all-gather.2.cloned.1.call-start = ((), (), s32[]{:S(2)}) async-start(), calls=%async_computation.4 | async-start | bytes 4456448 | tf_op jit(solution)/shard_map/all_gather | solution.py:175
  7.6 22.2 %copy-start = (f32[1,256,2,256]{3,1,2,0:T(8,128)}, f32[1,256,2,256]{3,1,2,0:T(8,128)S(1)}, u32[]{:S(2)}) copy-start(f32[1,256,2,256]{3,1,2,0:T(8,128)S(1)} %copy.12) | copy-start | bytes 1572868
  71.1 28.5 %all-to-all-start.2 = ((f32[32,6,8,256]{3,2,1,0:T(8,128)}), f32[32,6,8,256]{3,2,1,0:T(8,128)S(1)}, u32[]{:S(2)}, u32[]{:S(2)}) async-start(f32[32,6,8,256]{3,2,1,0:T(8,128)} %broadcast_in_dim.24), calls=%async_computation.2 | async-start | bytes 3145728 | tf_op jit(solution)/shard_map/all_to_all | solution.py:172
  99.6 1.7 %copy-start.2 = (f32[32,6,8,256]{3,2,1,0:T(8,128)}, f32[32,6,8,256]{3,2,1,0:T(8,128)S(1)}, u32[]{:S(2)}) copy-start(f32[32,6,8,256]{3,2,1,0:T(8,128)S(1)} %all-to-all-done.2.source_ref) | copy-start | bytes 4718596
  101.3 38.2 %all-to-all-start.3 = ((f32[32,3,2,8,256]{4,3,2,1,0:T(8,128)}), f32[32,3,2,8,256]{4,3,2,1,0:T(8,128)S(1)}, u32[]{:S(2)}, u32[]{:S(2)}) async-start(f32[32,3,2,8,256]{4,3,2,1,0:T(8,128)} %broadcast_in_dim.25), calls=%async_computation.3 | async-start | bytes 3145728 | tf_op jit(solution)/shard_map/all_to_all | solution.py:174
  139.5 1.2 copy-start.1
Sparse Core Ops, SparseCore 0:
  9.4 91.9 all-gather.1

commit v3 on v2

--- a/solution.py
+++ b/solution.py
@@ -8,6 +8,7 @@
 PANELS = 3
 W = 128
 NB = 256
+GROUP = 4
 N = PANELS * NB
 UPPER = [(r, c) for c in range(PANELS) for r in range(c + 1)]
 
@@ -117,18 +118,25 @@
         v_ref[m : m + W, 0:W] = -dot(v_ref[m : m + W, W:NB], cross)
 
 
-def update_kernel(place_ref, tops_ref, panel_ref, u_ref, v_ref, m_ref, o_ref, t_ref, p_ref, w_ref, y_ref, sems):
+def update_kernel(place_ref, tops_ref, held_ref, one_ref, two_ref, three_ref, u_ref, v_ref, m_ref, o_ref, t_ref, p_ref, w_ref, y_ref, sems):
     i, c = place_ref[0], place_ref[1]
-    arrivals = []
+    at = lax.rem(c, GROUP)
+    arrivals = [pltpu.make_async_copy(tops_ref.at[:, k], t_ref.at[:, k], sems.at[0, k]) for k in range(PANELS)]
+
+    def panel_copy(k, act):
+        for n, ref in enumerate([held_ref, one_ref, two_ref, three_ref]):
+
+            @pl.when(lax.rem(at + GROUP - k, GROUP) == n)
+            def _():
+                act(pltpu.make_async_copy(ref, p_ref.at[k], sems.at[1, k]))
+
     for k in range(PANELS):
-        arrivals.append(pltpu.make_async_copy(tops_ref.at[:, k], t_ref.at[:, k], sems.at[0, k]))
-        arrivals.append(pltpu.make_async_copy(panel_ref.at[k], p_ref.at[k], sems.at[1, k]))
-    for arrival in arrivals:
-        arrival.start()
+        arrivals[k].start()
+        panel_copy(k, lambda copy: copy.start())
     for k in range(PANELS):
         o = NB * k
-        arrivals[2 * k].wait()
-        arrivals[2 * k + 1].wait()
+        arrivals[k].wait()
+        panel_copy(k, lambda copy: copy.wait())
         t = jnp.concatenate([t_ref[:, k, n, :, :].reshape(NB, NB) for n in range(2)], 1)
         y = p_ref[k]
         if k:
@@ -158,6 +166,10 @@
     return jnp.broadcast_to(array[None], (count,) + array.shape)
 
 
+def send(array, axis, pairs):
+    return lax.ppermute(array, axis, pairs)
+
+
 def shards(matrix):
     rows_n = lax.axis_size("row")
     my_row = lax.axis_index("row")
@@ -165,14 +177,23 @@
     step = NB // rows_n
     cols_n = lax.axis_size("col")
     mine = matrix[0].transpose(1, 0, 2)
+    group = range(0, cols_n, GROUP)
+    near = send(mine[0], "col", [(g, g + GROUP) for g in range(PANELS)])
+    far = send(mine[0], "col", [(g, g + cols_n - GROUP) for g in range(PANELS)])
     pieces = mine.reshape(2, rows_n, step, NB).transpose(1, 0, 2, 3)
     pieces = lax.all_to_all(pieces, "row", 0, 0)[:PANELS]
     heads = lax.all_to_all(copies(pieces[:, 0], cols_n), "col", 0, 0)
+    heads, near = lax.optimization_barrier((heads, near))
+    middle = send(near, "col", [(GROUP + g, 2 * GROUP + g) for g in range(PANELS)])
     head = jnp.concatenate([heads[c, : c + 1] for c in range(PANELS)])
     lead = lax.all_to_all(copies(head, rows_n), "row", 0, 0)
-    lead, pieces = lax.optimization_barrier((lead, pieces))
+    held = jnp.where(my_col < GROUP, mine[0], near + middle + far)
+    lead, pieces, held = lax.optimization_barrier((lead, pieces, held))
+    shifted = [
+        send(held, "col", [(a + g, a + (g + n) % GROUP) for a in group for g in range(PANELS)])
+        for n in range(1, GROUP)
+    ]
     tops = lax.all_to_all(copies(pieces, rows_n), "row", 0, 0)
-    panel = lax.all_gather(mine[0], "col")
     f32 = jnp.float32
     hbm = pl.BlockSpec(memory_space=pltpu.HBM)
     upper, inverse = pl.pallas_call(
@@ -195,7 +216,7 @@
     out = pl.pallas_call(
         update_kernel,
         out_shape=jax.ShapeDtypeStruct((2, NB, NB), f32),
-        in_specs=[pl.BlockSpec(memory_space=pltpu.SMEM), hbm, hbm, vmem, vmem, vmem],
+        in_specs=[pl.BlockSpec(memory_space=pltpu.SMEM), hbm, hbm, hbm, hbm, hbm, vmem, vmem, vmem],
         out_specs=vmem,
         scratch_shapes=[
             pltpu.VMEM(tops.shape, f32),
@@ -206,7 +227,7 @@
         ],
         compiler_params=pltpu.CompilerParams(vmem_limit_bytes=56 << 20),
         cost_estimate=pl.CostEstimate(flops=2 << 30, bytes_accessed=8 << 20, transcendentals=0),
-    )(place, tops, panel, upper, inverse, mine)
+    )(place, tops, held, *shifted, upper, inverse, mine)
     return out.transpose(1, 0, 2)[None]
 
 

time: 161 us -> 161 us (level)
  starting transfers between devices: 10.1 us -> 54.3 us
  blocking collectives: 61.2 us -> 21.3 us
  between operations: 13.5 us -> 0.23 us
  waiting for transfers between devices: 22.7 us -> 31.5 us
    all_to_all x1 -> x0, blocking collectives: 39.9 us -> none  [shards(): heads = lax.all_to_all(copies(pieces[:, 0], cols_n), 'col', 0, 0)]
    ppermute x0 -> x6, waiting for transfers between devices: none -> 31.2 us  [send(): return lax.ppermute(array, axis, pairs)]
    ppermute x0 -> x6, starting transfers between devices: none -> 27.4 us  [send(): return lax.ppermute(array, axis, pairs)]
    all_to_all x1, waiting for transfers between devices: 22.7 us -> 0.35 us  [shards(): lead = lax.all_to_all(copies(head, rows_n), 'row', 0, 0)]
    all_to_all x0 -> x1, starting transfers between devices: none -> 13.7 us  [shards(): heads = lax.all_to_all(copies(pieces[:, 0], cols_n), 'col', 0, 0)]
    all_to_all x1, starting transfers between devices: 4.31 us -> 8.05 us  [shards(): tops = lax.all_to_all(copies(pieces, rows_n), 'row', 0, 0)]
  transfers between devices with their start and end apart: 3 -> 9, of which waited for: 1 -> 3; matrix products, arithmetic and copies ran while one was open for 2% -> 1% of each run, Pallas kernels for 21% -> 21%
where the time goes in v3:
time: 161 us
  starting transfers between devices  54.3 us (34%)
  Pallas kernels  44 us (27%)
  waiting for transfers between devices  31.5 us (20%)
  blocking collectives  21.3 us (13%)
  local copies, waits for them, and re-layouts  8.71 us (5%)
    pallas_call x1, Pallas kernels, shards(): pl.pallas_call(lead_kernel, out_shape=[jax.ShapeDtypeStruct((N, N), f32),...  33.2 us
    ppermute x6, waiting for transfers between devices, send(): return lax.ppermute(array, axis, pairs)  31.2 us
    ppermute x6, starting transfers between devices, send(): return lax.ppermute(array, axis, pairs)  27.4 us
    all_to_all x1, blocking collectives, shards(): pieces = lax.all_to_all(pieces, 'row', 0, 0)[:PANELS]  21.3 us
    all_to_all x1, starting transfers between devices, shards(): heads = lax.all_to_all(copies(pieces[:, 0], cols_n), 'col', 0, 0)  13.7 us
    pallas_call x1, Pallas kernels, shards(): pl.pallas_call(update_kernel, out_shape=jax.ShapeDtypeStruct((2, NB, NB),...  10.8 us
    all_to_all x1, starting transfers between devices, shards(): tops = lax.all_to_all(copies(pieces, rows_n), 'row', 0, 0)  8.05 us
    all_to_all x1, starting transfers between devices, shards(): lead = lax.all_to_all(copies(head, rows_n), 'row', 0, 0)  5.13 us
  transfers between devices with their start and end apart: 9, of which 3 were waited for; matrix products, arithmetic and copies ran while one was open for 1% of the time, Pallas kernels for 21%

profile of v3, /device:TPU:1, one launch (start us, length us, event | category | flops | bytes accessed | tf_op | source)
XLA Modules:
  0.0 160.7 jit_solution(7961743702669283016)
XLA Ops:
  0.0 1.1 copy.12
  1.1 0.0 copy-start
  1.1 0.1 copy.11
  1.2 21.3 %all_to_all.20 = f32[32,2,8,256]{3,2,1,0:T(8,128)S(1)} all-to-all(f32[32,2,8,256]{3,2,1,0:T(8,128)S(1)} %bitcast.32), channel_id=1, replica_groups=mesh['row'=32,'col'=16] {'row'}, dimensions={0} | all-to-all | bytes 1048576 | tf_op jit(solution)/shard_map/all_to_all | solution.py:184
  22.4 0.8 broadcast_in_dim.11
  23.2 13.7 %all-to-all-start.1 = ((f32[16,3,8,256]{3,2,1,0:T(8,128)}), f32[16,3,8,256]{3,2,1,0:T(8,128)S(1)}, u32[]{:S(2)}, u32[]{:S(2)}) async-start(f32[16,3,8,256]{3,2,1,0:T(8,128)} %broadcast_in_dim.11), calls=%async_computation.1 | async-start | bytes 786432 | tf_op jit(solution)/shard_map/all_to_all | solution.py:185
  36.9 0.7 slice_bitcast_fusion
  37.6 7.2 %collective-permute-start = (f32[256,256]{1,0:T(8,128)}, f32[256,256]{1,0:T(8,128)S(1)}, u32[]{:S(2)}, u32[]{:S(2)}) collective-permute-start(f32[256,256]{1,0:T(8,128)} %slice_bitcast_fusion), channel_id=1, source_target_pairs={{0,4},{1,5},{2,6},{16,20},{17,21},{18,22},{32,36},{33,37},{34,38},... | collective-permute-start | bytes 786440 | tf_op jit(solution)/shard_map/ppermute | solution.py:170
  44.8 15.0 %collective-permute-done = f32[256,256]{1,0:T(8,128)S(1)} collective-permute-done((f32[256,256]{1,0:T(8,128)}, f32[256,256]{1,0:T(8,128)S(1)}, u32[]{:S(2)}, u32[]{:S(2)}) %collective-permute-start) | collective-permute-done | bytes 262176 | tf_op jit(solution)/shard_map/ppermute | solution.py:170
  59.8 1.3 broadcast_in_dim.24
  61.2 5.1 %all-to-all-start.2 = ((f32[32,6,8,256]{3,2,1,0:T(8,128)}), f32[32,6,8,256]{3,2,1,0:T(8,128)S(1)}, u32[]{:S(2)}, u32[]{:S(2)}) async-start(f32[32,6,8,256]{3,2,1,0:T(8,128)} %broadcast_in_dim.24), calls=%async_computation.2 | async-start | bytes 3145728 | tf_op jit(solution)/shard_map/all_to_all | solution.py:189
  66.3 5.5 %collective-permute-start.2 = (f32[256,256]{1,0:T(8,128)}, f32[256,256]{1,0:T(8,128)S(1)}, u32[]{:S(2)}, u32[]{:S(2)}) collective-permute-start(f32[256,256]{1,0:T(8,128)} %slice_bitcast_fusion), channel_id=1, source_target_pairs={{0,12},{1,13},{2,14},{16,28},{17,29},{18,30},{32,44},{33,45},{34,4... | collective-permute-start | bytes 786440 | tf_op jit(solution)/shard_map/ppermute | solution.py:170
  71.8 0.7 collective-permute-start.1
  72.5 16.2 %collective-permute-done.2 = f32[256,256]{1,0:T(8,128)S(1)} collective-permute-done((f32[256,256]{1,0:T(8,128)}, f32[256,256]{1,0:T(8,128)S(1)}, u32[]{:S(2)}, u32[]{:S(2)}) %collective-permute-start.2) | collective-permute-done | bytes 262176 | tf_op jit(solution)/shard_map/ppermute | solution.py:170
  88.7 0.0 collective-permute-done.1
  88.7 0.1 add_select_fusion.held_ref
  88.7 0.4 all-to-all-done.2.source_ref
  89.1 1.5 broadcast_in_dim.25
  90.6 0.1 copy-done.1
  90.7 8.0 %all-to-all-start.3 = ((f32[32,3,2,8,256]{4,3,2,1,0:T(8,128)}), f32[32,3,2,8,256]{4,3,2,1,0:T(8,128)}, u32[]{:S(2)}, u32[]{:S(2)}) async-start(f32[32,3,2,8,256]{4,3,2,1,0:T(8,128)} %broadcast_in_dim.25), calls=%async_computation.3 | async-start | bytes 3145728 | tf_op jit(solution)/shard_map/all_to_all | solution.py:196
  98.8 2.0 %collective-permute-start.5 = (f32[256,256]{1,0:T(8,128)S(1)}, f32[256,256]{1,0:T(8,128)S(1)}, u32[]{:S(2)}, u32[]{:S(2)}) collective-permute-start(f32[256,256]{1,0:T(8,128)S(1)} %add_select_fusion.held_ref), channel_id=1, source_target_pairs={{0,3},{1,0},{2,1},{4,7},{5,4},{6,5},{8,11},{9,8},{10,9},{12,15},{1... | collective-permute-start | bytes 786440 | tf_op jit(solution)/shard_map/ppermute | solution.py:170
  100.8 10.6 %collective-permute-start.4 = (f32[256,256]{1,0:T(8,128)S(1)}, f32[256,256]{1,0:T(8,128)S(1)}, u32[]{:S(2)}, u32[]{:S(2)}) collective-permute-start(f32[256,256]{1,0:T(8,128)S(1)} %add_select_fusion.held_ref), channel_id=1, source_target_pairs={{0,2},{1,3},{2,0},{4,6},{5,7},{6,4},{8,10},{9,11},{10,8},{12,14},{... | collective-permute-start | bytes 786440 | tf_op jit(solution)/shard_map/ppermute | solution.py:170
  111.4 1.5 collective-permute-start.3
  112.9 0.6 pad_add_fusion.place_ref
  113.5 33.2 %shard_map.17 = (f32[768,768]{1,0:T(8,128)}, f32[768,256]{1,0:T(8,128)}) custom-call(f32[32,6,8,256]{3,2,1,0:T(8,128)} %copy-done.1), custom_call_target="tpu_custom_call" | custom-call | flops 2147483648 | bytes 104857600 | tf_op jit(solution)/shard_map/pallas_call | solution.py:199
  146.8 0.0 collective-permute-done.4.two_ref
  146.8 0.0 collective-permute-done.3.one_ref
  146.8 0.7 copy-done.3
  147.5 0.1 copy-done.4
  147.6 0.1 copy-done.5
  147.7 10.8 %shard_map.18 = f32[2,256,256]{2,1,0:T(8,128)} custom-call(s32[2]{0:T(128)} %pad_add_fusion.place_ref, f32[32,3,2,8,256]{4,3,2,1,0:T(8,128)} %all-to-all-done.3.tops_ref, f32[256,256]{1,0:T(8,128)} %copy-done.2, f32[256,256]{1,0:T(8,128)} %copy-done.5, f32[256,256]{1,0:T(8,128)} %copy-done.4, f32[256,256]{1,0:T(8,128)} %copy-done.3, ...), custom_call_target="tpu_custom_call" | custom-call | flops 2147483648 | bytes 8388608 | tf_op jit(solution)/shard_map/pallas_call | solution.py:216
  158.5 2.2 %copy.7 = f32[1,256,2,256]{3,2,1,0:T(2,128)} copy(f32[1,256,2,256]{3,1,2,0:T(8,128)} %bitcast.33) | data formatting | bytes 1048576 | tf_op jit(solution)/shard_map/broadcast_in_dim | solution.py:231
  (16 shorter events, 0.0 us)
Async XLA Ops:
  1.1 87.6 %copy-start = (f32[1,256,2,256]{3,1,2,0:T(8,128)}, f32[1,256,2,256]{3,1,2,0:T(8,128)S(1)}, u32[]{:S(2)}) copy-start(f32[1,256,2,256]{3,1,2,0:T(8,128)S(1)} %copy.12) | copy-start | bytes 1572868
  23.2 36.6 %all-to-all-start.1 = ((f32[16,3,8,256]{3,2,1,0:T(8,128)}), f32[16,3,8,256]{3,2,1,0:T(8,128)S(1)}, u32[]{:S(2)}, u32[]{:S(2)}) async-start(f32[16,3,8,256]{3,2,1,0:T(8,128)} %broadcast_in_dim.11), calls=%async_computation.1 | async-start | bytes 786432 | tf_op jit(solution)/shard_map/all_to_all | solution.py:185
  37.6 22.2 %collective-permute-start = (f32[256,256]{1,0:T(8,128)}, f32[256,256]{1,0:T(8,128)S(1)}, u32[]{:S(2)}, u32[]{:S(2)}) collective-permute-start(f32[256,256]{1,0:T(8,128)} %slice_bitcast_fusion), channel_id=1, source_target_pairs={{0,4},{1,5},{2,6},{16,20},{17,21},{18,22},{32,36},{33,37},{34,38},... | collective-permute-start | bytes 786440 | tf_op jit(solution)/shard_map/ppermute | solution.py:170
  61.2 27.9 %all-to-all-start.2 = ((f32[32,6,8,256]{3,2,1,0:T(8,128)}), f32[32,6,8,256]{3,2,1,0:T(8,128)S(1)}, u32[]{:S(2)}, u32[]{:S(2)}) async-start(f32[32,6,8,256]{3,2,1,0:T(8,128)} %broadcast_in_dim.24), calls=%async_computation.2 | async-start | bytes 3145728 | tf_op jit(solution)/shard_map/all_to_all | solution.py:189
  66.3 22.3 %collective-permute-start.2 = (f32[256,256]{1,0:T(8,128)}, f32[256,256]{1,0:T(8,128)S(1)}, u32[]{:S(2)}, u32[]{:S(2)}) collective-permute-start(f32[256,256]{1,0:T(8,128)} %slice_bitcast_fusion), channel_id=1, source_target_pairs={{0,12},{1,13},{2,14},{16,28},{17,29},{18,30},{32,44},{33,45},{34,4... | collective-permute-start | bytes 786440 | tf_op jit(solution)/shard_map/ppermute | solution.py:170
  71.8 16.9 %collective-permute-start.1 = (f32[256,256]{1,0:T(8,128)S(1)}, f32[256,256]{1,0:T(8,128)S(1)}, u32[]{:S(2)}, u32[]{:S(2)}) collective-permute-start(f32[256,256]{1,0:T(8,128)S(1)} %collective-permute-done), channel_id=1, source_target_pairs={{4,8},{5,9},{6,10},{20,24},{21,25},{22,26},{36,40},{37,41},{38,42}... | collective-permute-start | bytes 786440 | tf_op jit(solution)/shard_map/ppermute | solution.py:170
  88.7 22.7 %copy-start.2 = (f32[256,256]{1,0:T(8,128)}, f32[256,256]{1,0:T(8,128)S(1)}, u32[]{:S(2)}) copy-start(f32[256,256]{1,0:T(8,128)S(1)} %add_select_fusion.held_ref) | copy-start | bytes 786436
  89.1 1.6 %copy-start.1 = (f32[32,6,8,256]{3,2,1,0:T(8,128)}, f32[32,6,8,256]{3,2,1,0:T(8,128)S(1)}, u32[]{:S(2)}) copy-start(f32[32,6,8,256]{3,2,1,0:T(8,128)S(1)} %all-to-all-done.2.source_ref) | copy-start | bytes 4718596
  90.7 56.1 %all-to-all-start.3 = ((f32[32,3,2,8,256]{4,3,2,1,0:T(8,128)}), f32[32,3,2,8,256]{4,3,2,1,0:T(8,128)}, u32[]{:S(2)}, u32[]{:S(2)}) async-start(f32[32,3,2,8,256]{4,3,2,1,0:T(8,128)} %broadcast_in_dim.25), calls=%async_computation.3 | async-start | bytes 3145728 | tf_op jit(solution)/shard_map/all_to_all | solution.py:196
  98.8 48.0 %collective-permute-start.5 = (f32[256,256]{1,0:T(8,128)S(1)}, f32[256,256]{1,0:T(8,128)S(1)}, u32[]{:S(2)}, u32[]{:S(2)}) collective-permute-start(f32[256,256]{1,0:T(8,128)S(1)} %add_select_fusion.held_ref), channel_id=1, source_target_pairs={{0,3},{1,0},{2,1},{4,7},{5,4},{6,5},{8,11},{9,8},{10,9},{12,15},{1... | collective-permute-start | bytes 786440 | tf_op jit(solution)/shard_map/ppermute | solution.py:170
  100.8 46.0 %collective-permute-start.4 = (f32[256,256]{1,0:T(8,128)S(1)}, f32[256,256]{1,0:T(8,128)S(1)}, u32[]{:S(2)}, u32[]{:S(2)}) collective-permute-start(f32[256,256]{1,0:T(8,128)S(1)} %add_select_fusion.held_ref), channel_id=1, source_target_pairs={{0,2},{1,3},{2,0},{4,6},{5,7},{6,4},{8,10},{9,11},{10,8},{12,14},{... | collective-permute-start | bytes 786440 | tf_op jit(solution)/shard_map/ppermute | solution.py:170
  111.4 35.4 %collective-permute-start.3 = (f32[256,256]{1,0:T(8,128)S(1)}, f32[256,256]{1,0:T(8,128)S(1)}, u32[]{:S(2)}, u32[]{:S(2)}) collective-permute-start(f32[256,256]{1,0:T(8,128)S(1)} %add_select_fusion.held_ref), channel_id=1, source_target_pairs={{0,1},{1,2},{2,3},{4,5},{5,6},{6,7},{8,9},{9,10},{10,11},{12,13},{... | collective-permute-start | bytes 786440 | tf_op jit(solution)/shard_map/ppermute | solution.py:170
  146.8 0.7 copy-start.3
  146.8 0.8 copy-start.4
  146.8 0.9 copy-start.5

commit v4 on v2

--- a/solution.py
+++ b/solution.py
@@ -117,31 +117,24 @@
         v_ref[m : m + W, 0:W] = -dot(v_ref[m : m + W, W:NB], cross)
 
 
-def update_kernel(place_ref, tops_ref, panel_ref, u_ref, v_ref, m_ref, o_ref, t_ref, p_ref, w_ref, y_ref, sems):
+def update_kernel(place_ref, tops_ref, u_ref, v_ref, m_ref, o_ref, t_ref, w_ref, sems):
     i, c = place_ref[0], place_ref[1]
-    arrivals = []
-    for k in range(PANELS):
-        arrivals.append(pltpu.make_async_copy(tops_ref.at[:, k], t_ref.at[:, k], sems.at[0, k]))
-        arrivals.append(pltpu.make_async_copy(panel_ref.at[k], p_ref.at[k], sems.at[1, k]))
+    arrivals = [pltpu.make_async_copy(tops_ref.at[:, k], t_ref.at[:, k], sems.at[k]) for k in range(PANELS)]
     for arrival in arrivals:
         arrival.start()
     for k in range(PANELS):
         o = NB * k
-        arrivals[2 * k].wait()
-        arrivals[2 * k + 1].wait()
-        t = jnp.concatenate([t_ref[:, k, n, :, :].reshape(NB, NB) for n in range(2)], 1)
-        y = p_ref[k]
+        arrivals[k].wait()
+        t = jnp.concatenate([t_ref[:, k, n, :, :].reshape(NB, NB) for n in range(3)], 1)
         if k:
             t = t - dot(u_ref[0:o, o : o + NB], w_ref[0:o, :], 0, 0)
-            y = y - dot(y_ref[:, 0:o], u_ref[0:o, o : o + NB])
         w_ref[o : o + NB, :] = dot(v_ref[o : o + NB, :], t)
-        y_ref[:, o : o + NB] = dot(y, v_ref[o : o + NB, :], 1, 1)
 
     @pl.when(i < PANELS)
     def _():
-        y_ref[...] = u_ref[:, pl.ds(pl.multiple_of(jnp.minimum(i, PANELS - 1) * NB, NB), NB)].T
-
-    product = dot(y_ref[...], w_ref[...])
+        w_ref[:, 2 * NB :] = u_ref[:, pl.ds(pl.multiple_of(jnp.minimum(i, PANELS - 1) * NB, NB), NB)]
+
+    product = dot(w_ref[:, 2 * NB :], w_ref[:, : 2 * NB], 0, 0)
     keep = i >= PANELS
     o_ref[1] = jnp.where(keep, m_ref[1] - product[:, NB:], 0.0)
 
@@ -151,7 +144,7 @@
 
     @pl.when(c < PANELS)
     def _():
-        o_ref[0] = y_ref[:, pl.ds(pl.multiple_of(jnp.minimum(c, PANELS - 1) * NB, NB), NB)]
+        o_ref[0] = w_ref[pl.ds(pl.multiple_of(jnp.minimum(c, PANELS - 1) * NB, NB), NB), 2 * NB :].T
 
 
 def copies(array, count):
@@ -163,16 +156,16 @@
     my_row = lax.axis_index("row")
     my_col = lax.axis_index("col")
     step = NB // rows_n
-    cols_n = lax.axis_size("col")
     mine = matrix[0].transpose(1, 0, 2)
     pieces = mine.reshape(2, rows_n, step, NB).transpose(1, 0, 2, 3)
     pieces = lax.all_to_all(pieces, "row", 0, 0)[:PANELS]
-    heads = lax.all_to_all(copies(pieces[:, 0], cols_n), "col", 0, 0)
-    head = jnp.concatenate([heads[c, : c + 1] for c in range(PANELS)])
+    wide = lax.all_gather(pieces, "col")
+    head = jnp.concatenate([wide[c, : c + 1, 0] for c in range(PANELS)])
     lead = lax.all_to_all(copies(head, rows_n), "row", 0, 0)
-    lead, pieces = lax.optimization_barrier((lead, pieces))
-    tops = lax.all_to_all(copies(pieces, rows_n), "row", 0, 0)
-    panel = lax.all_gather(mine[0], "col")
+    lead, pieces, wide = lax.optimization_barrier((lead, pieces, wide))
+    theirs = wide.transpose(2, 0, 1, 3, 4).reshape(rows_n, PANELS, 1, step, NB)
+    tops = jnp.concatenate([copies(pieces, rows_n), theirs], 2)
+    tops = lax.all_to_all(tops, "row", 0, 0)
     f32 = jnp.float32
     hbm = pl.BlockSpec(memory_space=pltpu.HBM)
     upper, inverse = pl.pallas_call(
@@ -195,18 +188,12 @@
     out = pl.pallas_call(
         update_kernel,
         out_shape=jax.ShapeDtypeStruct((2, NB, NB), f32),
-        in_specs=[pl.BlockSpec(memory_space=pltpu.SMEM), hbm, hbm, vmem, vmem, vmem],
+        in_specs=[pl.BlockSpec(memory_space=pltpu.SMEM), hbm, vmem, vmem, vmem],
         out_specs=vmem,
-        scratch_shapes=[
-            pltpu.VMEM(tops.shape, f32),
-            pltpu.VMEM((PANELS, NB, NB), f32),
-            pltpu.VMEM((N, 2 * NB), f32),
-            pltpu.VMEM((NB, N), f32),
-            pltpu.SemaphoreType.DMA((2, PANELS)),
-        ],
+        scratch_shapes=[pltpu.VMEM(tops.shape, f32), pltpu.VMEM((N, 3 * NB), f32), pltpu.SemaphoreType.DMA((PANELS,))],
         compiler_params=pltpu.CompilerParams(vmem_limit_bytes=56 << 20),
         cost_estimate=pl.CostEstimate(flops=2 << 30, bytes_accessed=8 << 20, transcendentals=0),
-    )(place, tops, panel, upper, inverse, mine)
+    )(place, tops, upper, inverse, mine)
     return out.transpose(1, 0, 2)[None]
 
 

time: 161 us -> 143 us (0.89)
  blocking collectives: 61.2 us -> 86.9 us
  waiting for transfers between devices: 22.7 us -> 0.01 us
  between operations: 13.5 us -> 0.11 us
  starting transfers between devices: 10.1 us -> 3.84 us
  local copies, waits for them, and re-layouts: 8.34 us -> 5.2 us
  other arithmetic: 0.66 us -> 2.29 us
    all_gather x0 -> x1, blocking collectives: none -> 32.5 us  [shards(): wide = lax.all_gather(pieces, 'col')]
    all_to_all x2 -> x1, waiting for transfers between devices: 22.7 us -> 0.01 us  [shards(): tops = lax.all_to_all(tops, 'row', 0, 0)]
    all_to_all x1, blocking collectives: 39.9 us -> 33.2 us  [shards(): lead = lax.all_to_all(copies(head, rows_n), 'row', 0, 0)]
    all_to_all x2 -> x1, starting transfers between devices: 10.1 us -> 3.84 us  [shards(): tops = lax.all_to_all(tops, 'row', 0, 0)]
    broadcast_in_dim x4 -> x2, local copies, waits for them, and re-layouts: 2.89 us -> 0.35 us  [copies(): return jnp.broadcast_to(array[None], (count,) + array.shape)]
    concatenate x1 -> x2, other arithmetic: 0.01 us -> 1.63 us  [the longest x1 1.62 us: shards(): tops = jnp.concatenate([copies(pieces, rows_n), theirs], 2)]
  transfers between devices with their start and end apart: 3 -> 1, of which waited for: 1 -> 0; matrix products, arithmetic and copies ran while one was open for 2% -> 0% of each run, Pallas kernels for 21% -> 23%
where the time goes in v4:
time: 143 us; the launch traced here: 142 us
  blocking collectives  86.9 us (61%)
  Pallas kernels  43.9 us (31%)
  local copies, waits for them, and re-layouts  5.2 us (4%)
  starting transfers between devices  3.84 us (3%)
  other arithmetic  2.29 us (2%)
    pallas_call x1, Pallas kernels, shards(): pl.pallas_call(lead_kernel, out_shape=[jax.ShapeDtypeStruct((N, N), f32),...  33.2 us
    all_to_all x1, blocking collectives, shards(): lead = lax.all_to_all(copies(head, rows_n), 'row', 0, 0)  33.2 us
    all_gather x1, blocking collectives, shards(): wide = lax.all_gather(pieces, 'col')  32.5 us
    all_to_all x1, blocking collectives, shards(): pieces = lax.all_to_all(pieces, 'row', 0, 0)[:PANELS]  21.3 us
    pallas_call x1, Pallas kernels, shards(): pl.pallas_call(update_kernel, out_shape=jax.ShapeDtypeStruct((2, NB, NB),...  10.7 us
    all_to_all x1, starting transfers between devices, shards(): tops = lax.all_to_all(tops, 'row', 0, 0)  3.84 us
  transfers between devices with their start and end apart: 1, of which 0 were waited for; matrix products, arithmetic and copies ran while one was open for 0% of the time, Pallas kernels for 23%

profile of v4, /device:TPU:1, one launch (start us, length us, event | category | flops | bytes accessed | tf_op | source)
XLA Modules:
  0.0 142.2 jit_solution(17995497093890506201)
XLA Ops:
  0.0 1.1 copy.25
  1.1 0.0 copy-start.1
  1.1 0.1 copy.24
  1.2 21.3 %all_to_all.15 = f32[32,2,8,256]{3,2,1,0:T(8,128)S(1)} all-to-all(f32[32,2,8,256]{3,2,1,0:T(8,128)S(1)} %bitcast.37), channel_id=1, replica_groups=mesh['row'=32,'col'=16] {'row'}, dimensions={0} | all-to-all | bytes 1048576 | tf_op jit(solution)/shard_map/all_to_all | solution.py:161
  22.4 32.5 %all-gather = f32[48,2,8,256]{3,2,1,0:T(8,128)S(1)} all-gather(f32[3,2,8,256]{3,2,1,0:T(8,128)S(1)} %slice.16), channel_id=2, replica_groups=mesh['row'=32,'col'=16] {'col'}, dimensions={0}, use_global_device_ids=true | all-gather | bytes 835584 | tf_op jit(solution)/shard_map/all_gather | solution.py:162
  54.9 0.2 broadcast_in_dim.6
  55.1 0.0 copy-done.1
  55.1 33.2 %all_to_all.16.source_ref = f32[32,6,8,256]{3,2,1,0:T(8,128)} all-to-all(f32[32,6,8,256]{3,2,1,0:T(8,128)S(1)} %broadcast_in_dim.6), channel_id=1, replica_groups=mesh['row'=32,'col'=16] {'row'}, dimensions={0} | all-to-all | bytes 3145728 | tf_op jit(solution)/shard_map/all_to_all | solution.py:164
  88.2 0.1 copy.17
  88.3 0.2 broadcast_in_dim.7
  88.5 1.6 %pad_maximum_fusion = f32[32,3,3,8,256]{4,3,2,1,0:T(8,128)} fusion(f32[32,3,1,8,256]{4,3,2,1,0:T(8,128)S(1)} %bitcast.34, f32[32,3,2,8,256]{4,3,2,1,0:T(8,128)S(1)} %broadcast_in_dim.7), kind=kLoop, calls=%fused_computation | loop fusion | flops 589824 | bytes 4718592 | tf_op jit(solution)/shard_map/concatenate | solution.py:167
  90.1 3.8 %all-to-all-start.2 = ((f32[32,3,3,8,256]{4,3,2,1,0:T(8,128)}), f32[32,3,3,8,256]{4,3,2,1,0:T(8,128)S(1)}, u32[]{:S(2)}, u32[]{:S(2)}) async-start(f32[32,3,3,8,256]{4,3,2,1,0:T(8,128)} %pad_maximum_fusion), calls=%async_computation.2 | async-start | bytes 4718592 | tf_op jit(solution)/shard_map/all_to_all | solution.py:168
  94.0 0.7 pad_add_fusion.place_ref
  94.6 33.2 %shard_map.17 = (f32[768,768]{1,0:T(8,128)}, f32[768,256]{1,0:T(8,128)}) custom-call(f32[32,6,8,256]{3,2,1,0:T(8,128)} %all_to_all.16.source_ref), custom_call_target="tpu_custom_call" | custom-call | flops 2147483648 | bytes 104857600 | tf_op jit(solution)/shard_map/pallas_call | solution.py:171
  127.9 0.0 all-to-all-done.2.tops_ref
  127.9 0.0 copy-start
  127.9 1.4 copy-done
  129.3 10.7 %shard_map.18 = f32[2,256,256]{2,1,0:T(8,128)} custom-call(s32[2]{0:T(128)} %pad_add_fusion.place_ref, f32[32,3,3,8,256]{4,3,2,1,0:T(8,128)} %copy-done, f32[768,768]{1,0:T(8,128)} %get-tuple-element.13.u_ref, f32[768,256]{1,0:T(8,128)} %get-tuple-element.14.v_ref, f32[2,256,256]{2,1,0:T(8,128)} %bitcast.36), custom_call_target="tpu_custom_call" | custom-call | flops 2147483648 | bytes 8388608 | tf_op jit(solution)/shard_map/pallas_call | solution.py:188
  140.0 2.2 %copy.18 = f32[1,256,2,256]{3,2,1,0:T(2,128)} copy(f32[1,256,2,256]{3,1,2,0:T(8,128)} %bitcast.38) | data formatting | bytes 1048576 | tf_op jit(solution)/shard_map/broadcast_in_dim | solution.py:197
  (5 shorter events, 0.0 us)
Async XLA Ops:
  1.1 54.0 %copy-start.1 = (f32[1,256,2,256]{3,1,2,0:T(8,128)}, f32[1,256,2,256]{3,1,2,0:T(8,128)S(1)}, u32[]{:S(2)}) copy-start(f32[1,256,2,256]{3,1,2,0:T(8,128)S(1)} %copy.25) | copy-start | bytes 1572868
  90.1 37.8 %all-to-all-start.2 = ((f32[32,3,3,8,256]{4,3,2,1,0:T(8,128)}), f32[32,3,3,8,256]{4,3,2,1,0:T(8,128)S(1)}, u32[]{:S(2)}, u32[]{:S(2)}) async-start(f32[32,3,3,8,256]{4,3,2,1,0:T(8,128)} %pad_maximum_fusion), calls=%async_computation.2 | async-start | bytes 4718592 | tf_op jit(solution)/shard_map/all_to_all | solution.py:168
  127.9 1.4 copy-start

commit v5 on v4

--- a/solution.py
+++ b/solution.py
@@ -83,13 +83,13 @@
     arrival.start()
     u_ref[...] = jnp.zeros_like(u_ref)
     v_ref[...] = jnp.zeros_like(v_ref)
+    row_ref[...] = jnp.zeros_like(row_ref)
+    last_ref[...] = jnp.zeros_like(last_ref)
     arrival.wait()
     for n, (r, c) in enumerate(UPPER):
         s_ref[NB * r : NB * r + NB, NB * c : NB * c + NB] = a_ref[:, n, :, :].reshape(NB, NB)
     for r in range(1, PANELS):
         s_ref[NB * r : NB * r + NB, 0 : NB * r] = jnp.zeros((NB, NB * r), jnp.float32)
-    row_ref[...] = jnp.zeros_like(row_ref)
-    last_ref[...] = jnp.zeros_like(last_ref)
     d_ref[...] = s_ref[0:W, 0:W]
     lane = lax.broadcasted_iota(jnp.int32, (W, N), 1)
 
@@ -97,17 +97,32 @@
         o = pl.multiple_of(b * W, W)
         before = pl.multiple_of(jnp.maximum(b - 1, 0) * W, W)
         after = pl.multiple_of(jnp.minimum(b + 1, N // W - 1) * W, W)
+        second = lax.rem(b, 2) == 1
         rest = dot(last_ref[...], row_ref[...])
         u_ref[pl.ds(before, W), :] = jnp.where(lane >= o, rest, u_ref[pl.ds(before, W), :])
-        row_ref[...] = s_ref[pl.ds(o, W), :] - dot(u_ref[:, pl.ds(o, W)], u_ref[...], 0, 0)
-        ahead = u_ref[:, pl.ds(after, W)]
-        corner = s_ref[pl.ds(after, W), pl.ds(after, W)] - dot(ahead, ahead, 0, 0)
+        above = jnp.where(second, u_ref[pl.ds(before, W), pl.ds(o, W)], 0.0)
+        row_ref[...] = s_ref[pl.ds(o, W), :] - dot(above, u_ref[pl.ds(before, W), :], 0, 0)
         upper, inverse = factor(d_ref[...])
         u_ref[pl.ds(o, W), pl.ds(o, W)] = upper
         v_ref[pl.ds(o, W), pl.ds(pl.multiple_of((b % 2) * W, W), W)] = inverse
         last_ref[...] = inverse
-        beside = dot(inverse, row_ref[:, pl.ds(after, W)])
-        d_ref[...] = corner - dot(beside, beside, 0, 0)
+
+        @pl.when(jnp.logical_not(second))
+        def _():
+            beside = dot(inverse, row_ref[:, pl.ds(after, W)])
+            d_ref[...] = s_ref[pl.ds(after, W), pl.ds(after, W)] - dot(beside, beside, 0, 0)
+
+        for k in range(PANELS - 1):
+
+            @pl.when(b == 2 * k + 1)
+            def _():
+                e = NB * (k + 1)
+                u_ref[e - W : e, e:] = dot(inverse, row_ref[:, e:])
+                for f in range(e, N, NB):
+                    above = u_ref[e - NB : e, f : f + NB]
+                    s_ref[f : f + NB, f:] = s_ref[f : f + NB, f:] - dot(above, u_ref[e - NB : e, f:], 0, 0)
+                d_ref[...] = s_ref[e : e + W, e : e + W]
+
         return carry
 
     lax.fori_loop(0, N // W, body, 0)
@@ -117,14 +132,10 @@
         v_ref[m : m + W, 0:W] = -dot(v_ref[m : m + W, W:NB], cross)
 
 
-def update_kernel(place_ref, tops_ref, u_ref, v_ref, m_ref, o_ref, t_ref, w_ref, sems):
+def update_kernel(place_ref, t_ref, u_ref, v_ref, m_ref, o_ref, w_ref):
     i, c = place_ref[0], place_ref[1]
-    arrivals = [pltpu.make_async_copy(tops_ref.at[:, k], t_ref.at[:, k], sems.at[k]) for k in range(PANELS)]
-    for arrival in arrivals:
-        arrival.start()
     for k in range(PANELS):
         o = NB * k
-        arrivals[k].wait()
         t = jnp.concatenate([t_ref[:, k, n, :, :].reshape(NB, NB) for n in range(3)], 1)
         if k:
             t = t - dot(u_ref[0:o, o : o + NB], w_ref[0:o, :], 0, 0)
@@ -162,9 +173,10 @@
     wide = lax.all_gather(pieces, "col")
     head = jnp.concatenate([wide[c, : c + 1, 0] for c in range(PANELS)])
     lead = lax.all_to_all(copies(head, rows_n), "row", 0, 0)
-    lead, pieces, wide = lax.optimization_barrier((lead, pieces, wide))
     theirs = wide.transpose(2, 0, 1, 3, 4).reshape(rows_n, PANELS, 1, step, NB)
     tops = jnp.concatenate([copies(pieces, rows_n), theirs], 2)
+    place = jnp.stack([my_row, my_col]).astype(jnp.int32)
+    lead, tops, place = lax.optimization_barrier((lead, tops, place))
     tops = lax.all_to_all(tops, "row", 0, 0)
     f32 = jnp.float32
     hbm = pl.BlockSpec(memory_space=pltpu.HBM)
@@ -180,18 +192,17 @@
             pltpu.VMEM((W, W), f32),
             pltpu.SemaphoreType.DMA,
         ],
-        compiler_params=pltpu.CompilerParams(vmem_limit_bytes=56 << 20),
+        compiler_params=pltpu.CompilerParams(vmem_limit_bytes=55 << 20),
         cost_estimate=pl.CostEstimate(flops=2 << 30, bytes_accessed=100 << 20, transcendentals=0),
     )(lead)
-    place = jnp.stack([my_row, my_col]).astype(jnp.int32)
     vmem = pl.BlockSpec(memory_space=pltpu.VMEM)
     out = pl.pallas_call(
         update_kernel,
         out_shape=jax.ShapeDtypeStruct((2, NB, NB), f32),
-        in_specs=[pl.BlockSpec(memory_space=pltpu.SMEM), hbm, vmem, vmem, vmem],
+        in_specs=[pl.BlockSpec(memory_space=pltpu.SMEM), vmem, vmem, vmem, vmem],
         out_specs=vmem,
-        scratch_shapes=[pltpu.VMEM(tops.shape, f32), pltpu.VMEM((N, 3 * NB), f32), pltpu.SemaphoreType.DMA((PANELS,))],
-        compiler_params=pltpu.CompilerParams(vmem_limit_bytes=56 << 20),
+        scratch_shapes=[pltpu.VMEM((N, 3 * NB), f32)],
+        compiler_params=pltpu.CompilerParams(vmem_limit_bytes=24 << 20),
         cost_estimate=pl.CostEstimate(flops=2 << 30, bytes_accessed=8 << 20, transcendentals=0),
     )(place, tops, upper, inverse, mine)
     return out.transpose(1, 0, 2)[None]

time: 143 us -> 137 us (0.958)
  blocking collectives: 86.9 us -> 53.7 us
  waiting for transfers between devices: 0.01 us -> 26.4 us
  Pallas kernels: 43.9 us -> 32 us
  starting transfers between devices: 3.84 us -> 14.8 us
  local copies, waits for them, and re-layouts: 5.2 us -> 7.86 us
    all_to_all x1 -> x0, blocking collectives: 33.2 us -> none  [shards(): lead = lax.all_to_all(copies(head, rows_n), 'row', 0, 0)]
    all_to_all x0 -> x1, waiting for transfers between devices: none -> 20.7 us  [shards(): lead = lax.all_to_all(copies(head, rows_n), 'row', 0, 0)]
    all_to_all x0 -> x1, starting transfers between devices: none -> 10.4 us  [shards(): lead = lax.all_to_all(copies(head, rows_n), 'row', 0, 0)]
    pallas_call x1, Pallas kernels: 33.2 us -> 25.5 us  [shards(): pl.pallas_call(lead_kernel, out_shape=[jax.ShapeDtypeStruct((N, N), f32),...]
    all_to_all x1, waiting for transfers between devices: 0.01 us -> 5.66 us  [shards(): tops = lax.all_to_all(tops, 'row', 0, 0)]
    pallas_call x1, Pallas kernels: 10.7 us -> 6.47 us  [shards(): pl.pallas_call(update_kernel, out_shape=jax.ShapeDtypeStruct((2, NB, NB),...]
    unnamed x5 -> x7, local copies, waits for them, and re-layouts: 2.49 us -> 5.04 us
  transfers between devices with their start and end apart: 1 -> 2, of which waited for: 0 -> 2; matrix products, arithmetic and copies ran while one was open for 0% -> 1% of each run, Pallas kernels for 23% -> 19%
where the time goes in v5:
time: 137 us
  blocking collectives  53.7 us (39%)
  Pallas kernels  32 us (23%)
  waiting for transfers between devices  26.4 us (19%)
  starting transfers between devices  14.8 us (11%)
  local copies, waits for them, and re-layouts  7.86 us (6%)
  other arithmetic  1.69 us (1%)
    all_gather x1, blocking collectives, shards(): wide = lax.all_gather(pieces, 'col')  32.5 us
    pallas_call x1, Pallas kernels, shards(): pl.pallas_call(lead_kernel, out_shape=[jax.ShapeDtypeStruct((N, N), f32),...  25.5 us
    all_to_all x1, blocking collectives, shards(): pieces = lax.all_to_all(pieces, 'row', 0, 0)[:PANELS]  21.3 us
    all_to_all x1, waiting for transfers between devices, shards(): lead = lax.all_to_all(copies(head, rows_n), 'row', 0, 0)  20.7 us
    all_to_all x1, starting transfers between devices, shards(): lead = lax.all_to_all(copies(head, rows_n), 'row', 0, 0)  10.4 us
    pallas_call x1, Pallas kernels, shards(): pl.pallas_call(update_kernel, out_shape=jax.ShapeDtypeStruct((2, NB, NB),...  6.47 us
    all_to_all x1, waiting for transfers between devices, shards(): tops = lax.all_to_all(tops, 'row', 0, 0)  5.66 us
    unnamed x7, local copies, waits for them, and re-layouts  5.04 us
  transfers between devices with their start and end apart: 2, of which 2 were waited for; matrix products, arithmetic and copies ran while one was open for 1% of the time, Pallas kernels for 19%

profile of v5, /device:TPU:1, one launch (start us, length us, event | category | flops | bytes accessed | tf_op | source)
XLA Modules:
  0.0 136.5 jit_solution(2283515354057525126)
XLA Ops:
  0.0 1.1 copy.25
  1.1 0.1 copy.24
  1.1 21.3 %all_to_all.15 = f32[32,2,8,256]{3,2,1,0:T(8,128)S(1)} all-to-all(f32[32,2,8,256]{3,2,1,0:T(8,128)S(1)} %bitcast.38), channel_id=1, replica_groups=mesh['row'=32,'col'=16] {'row'}, dimensions={0} | all-to-all | bytes 1048576 | tf_op jit(solution)/shard_map/all_to_all | solution.py:172
  22.4 32.5 %all-gather = f32[48,2,8,256]{3,2,1,0:T(8,128)S(1)} all-gather(f32[3,2,8,256]{3,2,1,0:T(8,128)S(1)} %slice.16), channel_id=2, replica_groups=mesh['row'=32,'col'=16] {'col'}, dimensions={0}, use_global_device_ids=true | all-gather | bytes 835584 | tf_op jit(solution)/shard_map/all_gather | solution.py:173
  54.9 1.3 broadcast_in_dim.6
  56.2 10.4 %all-to-all-start.1 = ((f32[32,6,8,256]{3,2,1,0:T(8,128)}), f32[32,6,8,256]{3,2,1,0:T(8,128)S(1)}, u32[]{:S(2)}, u32[]{:S(2)}) async-start(f32[32,6,8,256]{3,2,1,0:T(8,128)} %broadcast_in_dim.6), calls=%async_computation.1 | async-start | bytes 3145728 | tf_op jit(solution)/shard_map/all_to_all | solution.py:175
  66.6 0.1 pad_add_fusion.place_ref
  66.7 0.1 copy.17
  66.7 0.2 broadcast_in_dim.7
  66.9 1.6 %pad_maximum_fusion = f32[32,3,3,8,256]{4,3,2,1,0:T(8,128)} fusion(f32[32,3,1,8,256]{4,3,2,1,0:T(8,128)S(1)} %bitcast.37, f32[32,3,2,8,256]{4,3,2,1,0:T(8,128)S(1)} %broadcast_in_dim.7), kind=kLoop, calls=%fused_computation | loop fusion | flops 589824 | bytes 4718592 | tf_op jit(solution)/shard_map/concatenate | solution.py:177
  68.5 20.7 %all-to-all-done.1.source_ref = f32[32,6,8,256]{3,2,1,0:T(8,128)S(1)} async-done(((f32[32,6,8,256]{3,2,1,0:T(8,128)}), f32[32,6,8,256]{3,2,1,0:T(8,128)S(1)}, u32[]{:S(2)}, u32[]{:S(2)}) %all-to-all-start.1) | async-done | bytes 1572896 | tf_op jit(solution)/shard_map/all_to_all | solution.py:175
  89.3 0.0 copy-start.2
  89.3 1.2 copy-done.2
  90.5 4.4 %all-to-all-start.2 = ((f32[32,3,3,8,256]{4,3,2,1,0:T(8,128)}), f32[32,3,3,8,256]{4,3,2,1,0:T(8,128)S(1)}, u32[]{:S(2)}, u32[]{:S(2)}) async-start(f32[32,3,3,8,256]{4,3,2,1,0:T(8,128)} %pad_maximum_fusion), calls=%async_computation.2 | async-start | bytes 4718592 | tf_op jit(solution)/shard_map/all_to_all | solution.py:180
  94.9 25.5 %shard_map.17 = (f32[768,768]{1,0:T(8,128)}, f32[768,256]{1,0:T(8,128)}) custom-call(f32[32,6,8,256]{3,2,1,0:T(8,128)} %copy-done.2), custom_call_target="tpu_custom_call" | custom-call | flops 2147483648 | bytes 104857600 | tf_op jit(solution)/shard_map/pallas_call | solution.py:183
  120.4 5.7 %all-to-all-done.2.t_ref = f32[32,3,3,8,256]{4,3,2,1,0:T(8,128)S(1)} async-done(((f32[32,3,3,8,256]{4,3,2,1,0:T(8,128)}), f32[32,3,3,8,256]{4,3,2,1,0:T(8,128)S(1)}, u32[]{:S(2)}, u32[]{:S(2)}) %all-to-all-start.2) | async-done | bytes 2359328 | tf_op jit(solution)/shard_map/all_to_all | solution.py:180
  126.1 0.0 copy-start
  126.1 1.7 %copy-done = f32[768,768]{1,0:T(8,128)S(1)} copy-done((f32[768,768]{1,0:T(8,128)S(1)}, f32[768,768]{1,0:T(8,128)}, u32[]{:S(2)}) %copy-start) | copy-done | bytes 2359320
  127.7 0.0 copy-start.1
  127.7 1.1 copy-done.1
  128.9 6.5 %shard_map.18 = f32[2,256,256]{2,1,0:T(8,128)S(1)} custom-call(s32[2]{0:T(128)S(1)} %pad_add_fusion.place_ref, f32[32,3,3,8,256]{4,3,2,1,0:T(8,128)S(1)} %all-to-all-done.2.t_ref, f32[768,768]{1,0:T(8,128)S(1)} %copy-done, f32[768,256]{1,0:T(8,128)S(1)} %copy-done.1, f32[2,256,256]{2,1,0:T(8,128)S(1)} %bitcast.31), custom_call_target="tpu_custom_call" | custom-call | flops 2147483648 | bytes 8388608 | tf_op jit(solution)/shard_map/pallas_call | solution.py:199
  135.3 1.2 copy.18
  (5 shorter events, 0.0 us)
Async XLA Ops:
  56.2 33.1 %all-to-all-start.1 = ((f32[32,6,8,256]{3,2,1,0:T(8,128)}), f32[32,6,8,256]{3,2,1,0:T(8,128)S(1)}, u32[]{:S(2)}, u32[]{:S(2)}) async-start(f32[32,6,8,256]{3,2,1,0:T(8,128)} %broadcast_in_dim.6), calls=%async_computation.1 | async-start | bytes 3145728 | tf_op jit(solution)/shard_map/all_to_all | solution.py:175
  89.3 1.2 copy-start.2
  90.5 35.6 %all-to-all-start.2 = ((f32[32,3,3,8,256]{4,3,2,1,0:T(8,128)}), f32[32,3,3,8,256]{4,3,2,1,0:T(8,128)S(1)}, u32[]{:S(2)}, u32[]{:S(2)}) async-start(f32[32,3,3,8,256]{4,3,2,1,0:T(8,128)} %pad_maximum_fusion), calls=%async_computation.2 | async-start | bytes 4718592 | tf_op jit(solution)/shard_map/all_to_all | solution.py:180
  126.1 1.7 %copy-start = (f32[768,768]{1,0:T(8,128)S(1)}, f32[768,768]{1,0:T(8,128)}, u32[]{:S(2)}) copy-start(f32[768,768]{1,0:T(8,128)} %get-tuple-element.13.u_ref) | copy-start | bytes 7077892
  127.7 1.1 copy-start.1

commit v6 on v5

--- a/solution.py
+++ b/solution.py
@@ -132,10 +132,23 @@
         v_ref[m : m + W, 0:W] = -dot(v_ref[m : m + W, W:NB], cross)
 
 
-def update_kernel(place_ref, t_ref, u_ref, v_ref, m_ref, o_ref, w_ref):
+def update_kernel(place_ref, t_ref, upper_ref, inverse_ref, m_ref, o_ref, w_ref, u_ref, v_ref, sems):
     i, c = place_ref[0], place_ref[1]
+    arrivals = []
     for k in range(PANELS):
         o = NB * k
+        rows, columns = pl.ds(o, NB), pl.ds(o, NB)
+        pair = (
+            pltpu.make_async_copy(inverse_ref.at[rows], v_ref.at[rows], sems.at[0, k]),
+            pltpu.make_async_copy(upper_ref.at[:, columns], u_ref.at[:, columns], sems.at[1, k]),
+        )
+        arrivals.append(pair)
+        for arrival in pair:
+            arrival.start()
+    for k in range(PANELS):
+        o = NB * k
+        for arrival in arrivals[k]:
+            arrival.wait()
         t = jnp.concatenate([t_ref[:, k, n, :, :].reshape(NB, NB) for n in range(3)], 1)
         if k:
             t = t - dot(u_ref[0:o, o : o + NB], w_ref[0:o, :], 0, 0)
@@ -199,12 +212,17 @@
     out = pl.pallas_call(
         update_kernel,
         out_shape=jax.ShapeDtypeStruct((2, NB, NB), f32),
-        in_specs=[pl.BlockSpec(memory_space=pltpu.SMEM), vmem, vmem, vmem, vmem],
+        in_specs=[pl.BlockSpec(memory_space=pltpu.SMEM), vmem, hbm, hbm, vmem],
         out_specs=vmem,
-        scratch_shapes=[pltpu.VMEM((N, 3 * NB), f32)],
+        scratch_shapes=[
+            pltpu.VMEM((N, 3 * NB), f32),
+            pltpu.VMEM((N, N), f32),
+            pltpu.VMEM((N, NB), f32),
+            pltpu.SemaphoreType.DMA((2, PANELS)),
+        ],
         compiler_params=pltpu.CompilerParams(vmem_limit_bytes=24 << 20),
         cost_estimate=pl.CostEstimate(flops=2 << 30, bytes_accessed=8 << 20, transcendentals=0),
-    )(place, tops, upper, inverse, mine)
+    )(place, tops, pltpu.with_memory_space_constraint(upper, pltpu.HBM), pltpu.with_memory_space_constraint(inverse, pltpu.HBM), mine)
     return out.transpose(1, 0, 2)[None]
 
 

time: 137 us -> 136 us (level)
  local copies, waits for them, and re-layouts: 7.86 us -> 5.04 us
  Pallas kernels: 32 us -> 34.1 us
    unnamed x7 -> x3, local copies, waits for them, and re-layouts: 5.04 us -> 2.24 us
    pallas_call x1, Pallas kernels: 6.47 us -> 8.52 us  [shards(): pl.pallas_call(update_kernel, out_shape=jax.ShapeDtypeStruct((2, NB, NB),...]
where the time goes in v6:
time: 136 us
  blocking collectives  53.7 us (39%)
  Pallas kernels  34.1 us (25%)
  waiting for transfers between devices  26.4 us (19%)
  starting transfers between devices  14.8 us (11%)
  local copies, waits for them, and re-layouts  5.04 us (4%)
  other arithmetic  1.7 us (1%)
    all_gather x1, blocking collectives, shards(): wide = lax.all_gather(pieces, 'col')  32.5 us
    pallas_call x1, Pallas kernels, shards(): pl.pallas_call(lead_kernel, out_shape=[jax.ShapeDtypeStruct((N, N), f32),...  25.5 us
    all_to_all x1, blocking collectives, shards(): pieces = lax.all_to_all(pieces, 'row', 0, 0)[:PANELS]  21.3 us
    all_to_all x1, waiting for transfers between devices, shards(): lead = lax.all_to_all(copies(head, rows_n), 'row', 0, 0)  20.7 us
    all_to_all x1, starting transfers between devices, shards(): lead = lax.all_to_all(copies(head, rows_n), 'row', 0, 0)  10.4 us
    pallas_call x1, Pallas kernels, shards(): pl.pallas_call(update_kernel, out_shape=jax.ShapeDtypeStruct((2, NB, NB),...  8.52 us
    all_to_all x1, waiting for transfers between devices, shards(): tops = lax.all_to_all(tops, 'row', 0, 0)  5.65 us
    all_to_all x1, starting transfers between devices, shards(): tops = lax.all_to_all(tops, 'row', 0, 0)  4.39 us
  transfers between devices with their start and end apart: 2, of which 2 were waited for; matrix products, arithmetic and copies ran while one was open for 1% of the time, Pallas kernels for 19%

profile of v6, /device:TPU:1, one launch (start us, length us, event | category | flops | bytes accessed | tf_op | source)
XLA Modules:
  0.0 135.8 jit_solution(10423842150315776683)
XLA Ops:
  0.0 1.1 copy.25
  1.1 0.1 copy.24
  1.1 21.3 %all_to_all.15 = f32[32,2,8,256]{3,2,1,0:T(8,128)S(1)} all-to-all(f32[32,2,8,256]{3,2,1,0:T(8,128)S(1)} %bitcast.38), channel_id=1, replica_groups=mesh['row'=32,'col'=16] {'row'}, dimensions={0} | all-to-all | bytes 1048576 | tf_op jit(solution)/shard_map/all_to_all | solution.py:185
  22.4 32.5 %all-gather = f32[48,2,8,256]{3,2,1,0:T(8,128)S(1)} all-gather(f32[3,2,8,256]{3,2,1,0:T(8,128)S(1)} %slice.16), channel_id=2, replica_groups=mesh['row'=32,'col'=16] {'col'}, dimensions={0}, use_global_device_ids=true | all-gather | bytes 835584 | tf_op jit(solution)/shard_map/all_gather | solution.py:186
  54.9 1.3 broadcast_in_dim.6
  56.2 10.4 %all-to-all-start.1 = ((f32[32,6,8,256]{3,2,1,0:T(8,128)}), f32[32,6,8,256]{3,2,1,0:T(8,128)S(1)}, u32[]{:S(2)}, u32[]{:S(2)}) async-start(f32[32,6,8,256]{3,2,1,0:T(8,128)} %broadcast_in_dim.6), calls=%async_computation.1 | async-start | bytes 3145728 | tf_op jit(solution)/shard_map/all_to_all | solution.py:188
  66.6 0.1 pad_add_fusion.place_ref
  66.7 0.1 copy.17
  66.7 0.2 broadcast_in_dim.7
  66.9 1.6 %pad_maximum_fusion = f32[32,3,3,8,256]{4,3,2,1,0:T(8,128)} fusion(f32[32,3,1,8,256]{4,3,2,1,0:T(8,128)S(1)} %bitcast.37, f32[32,3,2,8,256]{4,3,2,1,0:T(8,128)S(1)} %broadcast_in_dim.7), kind=kLoop, calls=%fused_computation | loop fusion | flops 589824 | bytes 4718592 | tf_op jit(solution)/shard_map/concatenate | solution.py:190
  68.5 20.7 %all-to-all-done.1.source_ref = f32[32,6,8,256]{3,2,1,0:T(8,128)S(1)} async-done(((f32[32,6,8,256]{3,2,1,0:T(8,128)}), f32[32,6,8,256]{3,2,1,0:T(8,128)S(1)}, u32[]{:S(2)}, u32[]{:S(2)}) %all-to-all-start.1) | async-done | bytes 1572896 | tf_op jit(solution)/shard_map/all_to_all | solution.py:188
  89.3 0.0 copy-start
  89.3 1.2 copy-done
  90.4 4.4 %all-to-all-start.2 = ((f32[32,3,3,8,256]{4,3,2,1,0:T(8,128)}), f32[32,3,3,8,256]{4,3,2,1,0:T(8,128)S(1)}, u32[]{:S(2)}, u32[]{:S(2)}) async-start(f32[32,3,3,8,256]{4,3,2,1,0:T(8,128)} %pad_maximum_fusion), calls=%async_computation.2 | async-start | bytes 4718592 | tf_op jit(solution)/shard_map/all_to_all | solution.py:193
  94.8 25.5 %shard_map.17 = (f32[768,768]{1,0:T(8,128)}, f32[768,256]{1,0:T(8,128)}) custom-call(f32[32,6,8,256]{3,2,1,0:T(8,128)} %copy-done), custom_call_target="tpu_custom_call" | custom-call | flops 2147483648 | bytes 104857600 | tf_op jit(solution)/shard_map/pallas_call | solution.py:196
  120.4 5.6 %all-to-all-done.2.t_ref = f32[32,3,3,8,256]{4,3,2,1,0:T(8,128)S(1)} async-done(((f32[32,3,3,8,256]{4,3,2,1,0:T(8,128)}), f32[32,3,3,8,256]{4,3,2,1,0:T(8,128)S(1)}, u32[]{:S(2)}, u32[]{:S(2)}) %all-to-all-start.2) | async-done | bytes 2359328 | tf_op jit(solution)/shard_map/all_to_all | solution.py:193
  126.0 8.5 %shard_map.18 = f32[2,256,256]{2,1,0:T(8,128)S(1)} custom-call(s32[2]{0:T(128)S(1)} %pad_add_fusion.place_ref, f32[32,3,3,8,256]{4,3,2,1,0:T(8,128)S(1)} %all-to-all-done.2.t_ref, f32[768,768]{1,0:T(8,128)} %get-tuple-element.13.upper_ref, f32[768,256]{1,0:T(8,128)} %get-tuple-element.14.inverse_ref, f32[2,256,256]{2,1,0:T(8,128)S(1)} %bitcast.31), custom_call_target="tpu_custom_call" | custom-call | flops 2147483648 | bytes 8388608 | tf_op jit(solution)/shard_map/pallas_call | solution.py:212
  134.6 1.2 copy.18
  (5 shorter events, 0.0 us)
Async XLA Ops:
  56.2 33.1 %all-to-all-start.1 = ((f32[32,6,8,256]{3,2,1,0:T(8,128)}), f32[32,6,8,256]{3,2,1,0:T(8,128)S(1)}, u32[]{:S(2)}, u32[]{:S(2)}) async-start(f32[32,6,8,256]{3,2,1,0:T(8,128)} %broadcast_in_dim.6), calls=%async_computation.1 | async-start | bytes 3145728 | tf_op jit(solution)/shard_map/all_to_all | solution.py:188
  89.3 1.2 copy-start
  90.4 35.6 %all-to-all-start.2 = ((f32[32,3,3,8,256]{4,3,2,1,0:T(8,128)}), f32[32,3,3,8,256]{4,3,2,1,0:T(8,128)S(1)}, u32[]{:S(2)}, u32[]{:S(2)}) async-start(f32[32,3,3,8,256]{4,3,2,1,0:T(8,128)} %pad_maximum_fusion), calls=%async_computation.2 | async-start | bytes 4718592 | tf_op jit(solution)/shard_map/all_to_all | solution.py:193

commit v7 on v6

--- a/solution.py
+++ b/solution.py
@@ -134,17 +134,23 @@
 
 def update_kernel(place_ref, t_ref, upper_ref, inverse_ref, m_ref, o_ref, w_ref, u_ref, v_ref, sems):
     i, c = place_ref[0], place_ref[1]
+    own = pl.ds(pl.multiple_of(jnp.minimum(i, PANELS - 1) * NB, NB), NB)
+    factors = pltpu.make_async_copy(upper_ref.at[:, own], u_ref.at[:, 0:NB], sems.at[1, 0])
     arrivals = []
     for k in range(PANELS):
         o = NB * k
-        rows, columns = pl.ds(o, NB), pl.ds(o, NB)
-        pair = (
-            pltpu.make_async_copy(inverse_ref.at[rows], v_ref.at[rows], sems.at[0, k]),
-            pltpu.make_async_copy(upper_ref.at[:, columns], u_ref.at[:, columns], sems.at[1, k]),
-        )
-        arrivals.append(pair)
-        for arrival in pair:
+        arrivals.append([pltpu.make_async_copy(inverse_ref.at[o : o + NB], v_ref.at[o : o + NB], sems.at[0, k])])
+        if k:
+            arrivals[k].append(
+                pltpu.make_async_copy(upper_ref.at[0:o, o : o + NB], u_ref.at[0:o, o : o + NB], sems.at[1, k])
+            )
+        for arrival in arrivals[k]:
             arrival.start()
+
+    @pl.when(i < PANELS)
+    def _():
+        factors.start()
+
     for k in range(PANELS):
         o = NB * k
         for arrival in arrivals[k]:
@@ -156,7 +162,8 @@
 
     @pl.when(i < PANELS)
     def _():
-        w_ref[:, 2 * NB :] = u_ref[:, pl.ds(pl.multiple_of(jnp.minimum(i, PANELS - 1) * NB, NB), NB)]
+        factors.wait()
+        w_ref[:, 2 * NB :] = u_ref[:, 0:NB]
 
     product = dot(w_ref[:, 2 * NB :], w_ref[:, : 2 * NB], 0, 0)
     keep = i >= PANELS

time: 136 us -> 136 us (level)
  no operation moved by 1% of the time
where the time goes in v7:
time: 136 us
  blocking collectives  53.7 us (39%)
  Pallas kernels  33.8 us (25%)
  waiting for transfers between devices  26.4 us (19%)
  starting transfers between devices  14.8 us (11%)
  local copies, waits for them, and re-layouts  5.04 us (4%)
  other arithmetic  1.7 us (1%)
    all_gather x1, blocking collectives, shards(): wide = lax.all_gather(pieces, 'col')  32.5 us
    pallas_call x1, Pallas kernels, shards(): pl.pallas_call(lead_kernel, out_shape=[jax.ShapeDtypeStruct((N, N), f32),...  25.5 us
    all_to_all x1, blocking collectives, shards(): pieces = lax.all_to_all(pieces, 'row', 0, 0)[:PANELS]  21.3 us
    all_to_all x1, waiting for transfers between devices, shards(): lead = lax.all_to_all(copies(head, rows_n), 'row', 0, 0)  20.7 us
    all_to_all x1, starting transfers between devices, shards(): lead = lax.all_to_all(copies(head, rows_n), 'row', 0, 0)  10.4 us
    pallas_call x1, Pallas kernels, shards(): pl.pallas_call(update_kernel, out_shape=jax.ShapeDtypeStruct((2, NB, NB),...  8.26 us
    all_to_all x1, waiting for transfers between devices, shards(): tops = lax.all_to_all(tops, 'row', 0, 0)  5.65 us
    all_to_all x1, starting transfers between devices, shards(): tops = lax.all_to_all(tops, 'row', 0, 0)  4.39 us
  transfers between devices with their start and end apart: 2, of which 2 were waited for; matrix products, arithmetic and copies ran while one was open for 1% of the time, Pallas kernels for 19%

profile of v7, /device:TPU:1, one launch (start us, length us, event | category | flops | bytes accessed | tf_op | source)
XLA Modules:
  0.0 135.5 jit_solution(12490379684475052041)
XLA Ops:
  0.0 1.1 copy.25
  1.1 0.1 copy.24
  1.1 21.3 %all_to_all.15 = f32[32,2,8,256]{3,2,1,0:T(8,128)S(1)} all-to-all(f32[32,2,8,256]{3,2,1,0:T(8,128)S(1)} %bitcast.38), channel_id=1, replica_groups=mesh['row'=32,'col'=16] {'row'}, dimensions={0} | all-to-all | bytes 1048576 | tf_op jit(solution)/shard_map/all_to_all | solution.py:192
  22.4 32.5 %all-gather = f32[48,2,8,256]{3,2,1,0:T(8,128)S(1)} all-gather(f32[3,2,8,256]{3,2,1,0:T(8,128)S(1)} %slice.16), channel_id=2, replica_groups=mesh['row'=32,'col'=16] {'col'}, dimensions={0}, use_global_device_ids=true | all-gather | bytes 835584 | tf_op jit(solution)/shard_map/all_gather | solution.py:193
  54.9 1.3 broadcast_in_dim.6
  56.2 10.4 %all-to-all-start.1 = ((f32[32,6,8,256]{3,2,1,0:T(8,128)}), f32[32,6,8,256]{3,2,1,0:T(8,128)S(1)}, u32[]{:S(2)}, u32[]{:S(2)}) async-start(f32[32,6,8,256]{3,2,1,0:T(8,128)} %broadcast_in_dim.6), calls=%async_computation.1 | async-start | bytes 3145728 | tf_op jit(solution)/shard_map/all_to_all | solution.py:195
  66.6 0.1 pad_add_fusion.place_ref
  66.7 0.1 copy.17
  66.7 0.2 broadcast_in_dim.7
  66.9 1.6 %pad_maximum_fusion = f32[32,3,3,8,256]{4,3,2,1,0:T(8,128)} fusion(f32[32,3,1,8,256]{4,3,2,1,0:T(8,128)S(1)} %bitcast.37, f32[32,3,2,8,256]{4,3,2,1,0:T(8,128)S(1)} %broadcast_in_dim.7), kind=kLoop, calls=%fused_computation | loop fusion | flops 589824 | bytes 4718592 | tf_op jit(solution)/shard_map/concatenate | solution.py:197
  68.5 20.7 %all-to-all-done.1.source_ref = f32[32,6,8,256]{3,2,1,0:T(8,128)S(1)} async-done(((f32[32,6,8,256]{3,2,1,0:T(8,128)}), f32[32,6,8,256]{3,2,1,0:T(8,128)S(1)}, u32[]{:S(2)}, u32[]{:S(2)}) %all-to-all-start.1) | async-done | bytes 1572896 | tf_op jit(solution)/shard_map/all_to_all | solution.py:195
  89.3 0.0 copy-start
  89.3 1.2 copy-done
  90.4 4.4 %all-to-all-start.2 = ((f32[32,3,3,8,256]{4,3,2,1,0:T(8,128)}), f32[32,3,3,8,256]{4,3,2,1,0:T(8,128)S(1)}, u32[]{:S(2)}, u32[]{:S(2)}) async-start(f32[32,3,3,8,256]{4,3,2,1,0:T(8,128)} %pad_maximum_fusion), calls=%async_computation.2 | async-start | bytes 4718592 | tf_op jit(solution)/shard_map/all_to_all | solution.py:200
  94.8 25.5 %shard_map.17 = (f32[768,768]{1,0:T(8,128)}, f32[768,256]{1,0:T(8,128)}) custom-call(f32[32,6,8,256]{3,2,1,0:T(8,128)} %copy-done), custom_call_target="tpu_custom_call" | custom-call | flops 2147483648 | bytes 104857600 | tf_op jit(solution)/shard_map/pallas_call | solution.py:203
  120.4 5.6 %all-to-all-done.2.t_ref = f32[32,3,3,8,256]{4,3,2,1,0:T(8,128)S(1)} async-done(((f32[32,3,3,8,256]{4,3,2,1,0:T(8,128)}), f32[32,3,3,8,256]{4,3,2,1,0:T(8,128)S(1)}, u32[]{:S(2)}, u32[]{:S(2)}) %all-to-all-start.2) | async-done | bytes 2359328 | tf_op jit(solution)/shard_map/all_to_all | solution.py:200
  126.0 8.3 %shard_map.18 = f32[2,256,256]{2,1,0:T(8,128)S(1)} custom-call(s32[2]{0:T(128)S(1)} %pad_add_fusion.place_ref, f32[32,3,3,8,256]{4,3,2,1,0:T(8,128)S(1)} %all-to-all-done.2.t_ref, f32[768,768]{1,0:T(8,128)} %get-tuple-element.13.upper_ref, f32[768,256]{1,0:T(8,128)} %get-tuple-element.14.inverse_ref, f32[2,256,256]{2,1,0:T(8,128)S(1)} %bitcast.31), custom_call_target="tpu_custom_call" | custom-call | flops 2147483648 | bytes 8388608 | tf_op jit(solution)/shard_map/pallas_call | solution.py:219
  134.3 1.2 copy.18
  (5 shorter events, 0.0 us)
Async XLA Ops:
  56.2 33.1 %all-to-all-start.1 = ((f32[32,6,8,256]{3,2,1,0:T(8,128)}), f32[32,6,8,256]{3,2,1,0:T(8,128)S(1)}, u32[]{:S(2)}, u32[]{:S(2)}) async-start(f32[32,6,8,256]{3,2,1,0:T(8,128)} %broadcast_in_dim.6), calls=%async_computation.1 | async-start | bytes 3145728 | tf_op jit(solution)/shard_map/all_to_all | solution.py:195
  89.3 1.2 copy-start
  90.4 35.6 %all-to-all-start.2 = ((f32[32,3,3,8,256]{4,3,2,1,0:T(8,128)}), f32[32,3,3,8,256]{4,3,2,1,0:T(8,128)S(1)}, u32[]{:S(2)}, u32[]{:S(2)}) async-start(f32[32,3,3,8,256]{4,3,2,1,0:T(8,128)} %pad_maximum_fusion), calls=%async_computation.2 | async-start | bytes 4718592 | tf_op jit(solution)/shard_map/all_to_all | solution.py:200

commit v8 on v7

--- a/solution.py
+++ b/solution.py
@@ -78,16 +78,24 @@
     return jnp.concatenate(upper, 0), jnp.concatenate(inverse, 0)
 
 
-def lead_kernel(source_ref, u_ref, v_ref, a_ref, s_ref, d_ref, row_ref, last_ref, sem):
-    arrival = pltpu.make_async_copy(source_ref, a_ref, sem)
-    arrival.start()
+def lead_kernel(place_ref, mine_ref, other_ref, u_ref, v_ref, a_ref, s_ref, d_ref, row_ref, last_ref, sems):
+    half = lax.rem(place_ref[0], 2)
+    arrivals = [
+        pltpu.make_async_copy(mine_ref, a_ref.at[half], sems.at[0]),
+        pltpu.make_async_copy(other_ref, a_ref.at[1 - half], sems.at[1]),
+    ]
+    for arrival in arrivals:
+        arrival.start()
     u_ref[...] = jnp.zeros_like(u_ref)
     v_ref[...] = jnp.zeros_like(v_ref)
     row_ref[...] = jnp.zeros_like(row_ref)
     last_ref[...] = jnp.zeros_like(last_ref)
-    arrival.wait()
+    for arrival in arrivals:
+        arrival.wait()
     for n, (r, c) in enumerate(UPPER):
-        s_ref[NB * r : NB * r + NB, NB * c : NB * c + NB] = a_ref[:, n, :, :].reshape(NB, NB)
+        for h in range(2):
+            o = NB * c + W * h
+            s_ref[NB * r : NB * r + NB, o : o + W] = a_ref[h, :, n, :, :].reshape(NB, W)
     for r in range(1, PANELS):
         s_ref[NB * r : NB * r + NB, 0 : NB * r] = jnp.zeros((NB, NB * r), jnp.float32)
     d_ref[...] = s_ref[0:W, 0:W]
@@ -192,29 +200,32 @@
     pieces = lax.all_to_all(pieces, "row", 0, 0)[:PANELS]
     wide = lax.all_gather(pieces, "col")
     head = jnp.concatenate([wide[c, : c + 1, 0] for c in range(PANELS)])
-    lead = lax.all_to_all(copies(head, rows_n), "row", 0, 0)
+    halves = head.reshape(len(UPPER), step, 2, W).transpose(2, 0, 1, 3)
+    lead = copies(halves, rows_n // 2).reshape(rows_n, len(UPPER), step, W)
+    lead = lax.all_to_all(lead, "row", 0, 0)
     theirs = wide.transpose(2, 0, 1, 3, 4).reshape(rows_n, PANELS, 1, step, NB)
     tops = jnp.concatenate([copies(pieces, rows_n), theirs], 2)
     place = jnp.stack([my_row, my_col]).astype(jnp.int32)
     lead, tops, place = lax.optimization_barrier((lead, tops, place))
     tops = lax.all_to_all(tops, "row", 0, 0)
+    other = lax.ppermute(lead, "row", [(i, i ^ 1) for i in range(rows_n)])
     f32 = jnp.float32
     hbm = pl.BlockSpec(memory_space=pltpu.HBM)
     upper, inverse = pl.pallas_call(
         lead_kernel,
         out_shape=[jax.ShapeDtypeStruct((N, N), f32), jax.ShapeDtypeStruct((N, NB), f32)],
-        in_specs=[hbm],
+        in_specs=[pl.BlockSpec(memory_space=pltpu.SMEM), hbm, hbm],
         scratch_shapes=[
-            pltpu.VMEM(lead.shape, f32),
+            pltpu.VMEM((2,) + lead.shape, f32),
             pltpu.VMEM((N, N), f32),
             pltpu.VMEM((W, W), f32),
             pltpu.VMEM((W, N), f32),
             pltpu.VMEM((W, W), f32),
-            pltpu.SemaphoreType.DMA,
+            pltpu.SemaphoreType.DMA((2,)),
         ],
         compiler_params=pltpu.CompilerParams(vmem_limit_bytes=55 << 20),
         cost_estimate=pl.CostEstimate(flops=2 << 30, bytes_accessed=100 << 20, transcendentals=0),
-    )(lead)
+    )(place, lead, other)
     vmem = pl.BlockSpec(memory_space=pltpu.VMEM)
     out = pl.pallas_call(
         update_kernel,

time: 136 us -> 127 us (0.934)
  waiting for transfers between devices: 26.4 us -> 14 us
  starting transfers between devices: 14.8 us -> 16.4 us
    all_to_all x1, waiting for transfers between devices: 20.7 us -> 11.7 us  [shards(): lead = lax.all_to_all(lead, 'row', 0, 0)]
    all_to_all x1, waiting for transfers between devices: 5.65 us -> 0.01 us  [shards(): tops = lax.all_to_all(tops, 'row', 0, 0)]
    ppermute x0 -> x1, waiting for transfers between devices: none -> 2.25 us  [shards(): other = lax.ppermute(lead, 'row', [(i, i ^ 1) for i in range(rows_n)])]
    ppermute x0 -> x1, starting transfers between devices: none -> 2.13 us  [shards(): other = lax.ppermute(lead, 'row', [(i, i ^ 1) for i in range(rows_n)])]
    unnamed x3 -> x7, local copies, waits for them, and re-layouts: 2.24 us -> 2.87 us
  transfers between devices with their start and end apart: 2 -> 3, of which waited for: 2 -> 2; matrix products, arithmetic and copies ran while one was open for 1% -> 2% of each run, Pallas kernels for 19% -> 21%
where the time goes in v8:
time: 127 us; the launch traced here: 126 us
  blocking collectives  53.7 us (42%)
  Pallas kernels  34.5 us (27%)
  starting transfers between devices  16.4 us (13%)
  waiting for transfers between devices  14 us (11%)
  local copies, waits for them, and re-layouts  5.32 us (4%)
  other arithmetic  2.28 us (2%)
    all_gather x1, blocking collectives, shards(): wide = lax.all_gather(pieces, 'col')  32.5 us
    pallas_call x1, Pallas kernels, shards(): pl.pallas_call(lead_kernel, out_shape=[jax.ShapeDtypeStruct((N, N), f32),...  26.2 us
    all_to_all x1, blocking collectives, shards(): pieces = lax.all_to_all(pieces, 'row', 0, 0)[:PANELS]  21.3 us
    all_to_all x1, waiting for transfers between devices, shards(): lead = lax.all_to_all(lead, 'row', 0, 0)  11.7 us
    all_to_all x1, starting transfers between devices, shards(): lead = lax.all_to_all(lead, 'row', 0, 0)  10.4 us
    pallas_call x1, Pallas kernels, shards(): pl.pallas_call(update_kernel, out_shape=jax.ShapeDtypeStruct((2, NB, NB),...  8.26 us
    all_to_all x1, starting transfers between devices, shards(): tops = lax.all_to_all(tops, 'row', 0, 0)  3.84 us
    unnamed x7, local copies, waits for them, and re-layouts  2.87 us
  transfers between devices with their start and end apart: 3, of which 2 were waited for; matrix products, arithmetic and copies ran while one was open for 2% of the time, Pallas kernels for 21%

profile of v8, /device:TPU:1, one launch (start us, length us, event | category | flops | bytes accessed | tf_op | source)
XLA Modules:
  0.0 126.3 jit_solution(18228905859642379783)
XLA Ops:
  0.0 1.1 copy.28
  1.1 0.1 copy.27
  1.1 21.3 %all_to_all.15 = f32[32,2,8,256]{3,2,1,0:T(8,128)S(1)} all-to-all(f32[32,2,8,256]{3,2,1,0:T(8,128)S(1)} %bitcast.41), channel_id=1, replica_groups=mesh['row'=32,'col'=16] {'row'}, dimensions={0} | all-to-all | bytes 1048576 | tf_op jit(solution)/shard_map/all_to_all | solution.py:200
  22.4 32.5 %all-gather = f32[48,2,8,256]{3,2,1,0:T(8,128)S(1)} all-gather(f32[3,2,8,256]{3,2,1,0:T(8,128)S(1)} %slice.16), channel_id=2, replica_groups=mesh['row'=32,'col'=16] {'col'}, dimensions={0}, use_global_device_ids=true | all-gather | bytes 835584 | tf_op jit(solution)/shard_map/all_gather | solution.py:201
  54.9 1.0 broadcast_in_dim.6
  55.8 10.4 %all-to-all-start.1 = ((f32[32,6,8,128]{3,2,1,0:T(8,128)}), f32[32,6,8,128]{3,2,1,0:T(8,128)S(1)}, u32[]{:S(2)}, u32[]{:S(2)}) async-start(f32[32,6,8,128]{3,2,1,0:T(8,128)} %bitcast.10), calls=%async_computation.1 | async-start | bytes 1572864 | tf_op jit(solution)/shard_map/all_to_all | solution.py:205
  66.2 0.7 pad_add_fusion.place_ref
  66.9 0.1 copy.18
  66.9 0.2 broadcast_in_dim.7
  67.1 1.6 %pad_maximum_fusion = f32[32,3,3,8,256]{4,3,2,1,0:T(8,128)} fusion(f32[32,3,1,8,256]{4,3,2,1,0:T(8,128)S(1)} %bitcast.40, f32[32,3,2,8,256]{4,3,2,1,0:T(8,128)S(1)} %broadcast_in_dim.7), kind=kLoop, calls=%fused_computation | loop fusion | flops 589824 | bytes 4718592 | tf_op jit(solution)/shard_map/concatenate | solution.py:207
  68.8 11.7 %all-to-all-done.1.mine_ref = f32[32,6,8,128]{3,2,1,0:T(8,128)S(1)} async-done(((f32[32,6,8,128]{3,2,1,0:T(8,128)}), f32[32,6,8,128]{3,2,1,0:T(8,128)S(1)}, u32[]{:S(2)}, u32[]{:S(2)}) %all-to-all-start.1) | async-done | bytes 786464 | tf_op jit(solution)/shard_map/all_to_all | solution.py:205
  80.5 0.0 copy-start.1
  80.5 0.9 copy-done.1
  81.4 3.8 %all-to-all-start.2 = ((f32[32,3,3,8,256]{4,3,2,1,0:T(8,128)}), f32[32,3,3,8,256]{4,3,2,1,0:T(8,128)S(1)}, u32[]{:S(2)}, u32[]{:S(2)}) async-start(f32[32,3,3,8,256]{4,3,2,1,0:T(8,128)} %pad_maximum_fusion), calls=%async_computation.2 | async-start | bytes 4718592 | tf_op jit(solution)/shard_map/all_to_all | solution.py:210
  85.2 0.0 copy-start
  85.2 2.1 %collective-permute-start = (f32[32,6,8,128]{3,2,1,0:T(8,128)}, f32[32,6,8,128]{3,2,1,0:T(8,128)S(1)}, u32[]{:S(2)}, u32[]{:S(2)}) collective-permute-start(f32[32,6,8,128]{3,2,1,0:T(8,128)} %copy-done.1), channel_id=1, source_target_pairs={{0,16},{16,0},{32,48},{48,32},{64,80},{80,64},{96,112},{112,96},{1... | collective-permute-start | bytes 2359304 | tf_op jit(solution)/shard_map/ppermute | solution.py:211
  87.4 2.3 %collective-permute-done.other_ref = f32[32,6,8,128]{3,2,1,0:T(8,128)S(1)} collective-permute-done((f32[32,6,8,128]{3,2,1,0:T(8,128)}, f32[32,6,8,128]{3,2,1,0:T(8,128)S(1)}, u32[]{:S(2)}, u32[]{:S(2)}) %collective-permute-start) | collective-permute-done | bytes 786464 | tf_op jit(solution)/shard_map/ppermute | solution.py:211
  89.6 0.0 copy-start.2
  89.6 0.9 copy-done.2
  90.5 26.2 %shard_map.17 = (f32[768,768]{1,0:T(8,128)}, f32[768,256]{1,0:T(8,128)}) custom-call(s32[2]{0:T(128)} %pad_add_fusion.place_ref, f32[32,6,8,128]{3,2,1,0:T(8,128)} %copy-done.1, f32[32,6,8,128]{3,2,1,0:T(8,128)} %copy-done.2), custom_call_target="tpu_custom_call" | custom-call | flops 2147483648 | bytes 104857600 | tf_op jit(solution)/shard_map/pallas_call | solution.py:214
  116.8 0.0 all-to-all-done.2.t_ref
  116.8 0.0 copy-done
  116.8 8.3 %shard_map.18 = f32[2,256,256]{2,1,0:T(8,128)S(1)} custom-call(s32[2]{0:T(128)S(1)} %copy-done, f32[32,3,3,8,256]{4,3,2,1,0:T(8,128)S(1)} %all-to-all-done.2.t_ref, f32[768,768]{1,0:T(8,128)} %get-tuple-element.13.upper_ref, f32[768,256]{1,0:T(8,128)} %get-tuple-element.14.inverse_ref, f32[2,256,256]{2,1,0:T(8,128)S(1)} %bitcast.34), custom_call_target="tpu_custom_call" | custom-call | flops 2147483648 | bytes 8388608 | tf_op jit(solution)/shard_map/pallas_call | solution.py:230
  125.1 1.2 copy.19
  (4 shorter events, 0.0 us)
Async XLA Ops:
  55.8 24.6 %all-to-all-start.1 = ((f32[32,6,8,128]{3,2,1,0:T(8,128)}), f32[32,6,8,128]{3,2,1,0:T(8,128)S(1)}, u32[]{:S(2)}, u32[]{:S(2)}) async-start(f32[32,6,8,128]{3,2,1,0:T(8,128)} %bitcast.10), calls=%async_computation.1 | async-start | bytes 1572864 | tf_op jit(solution)/shard_map/all_to_all | solution.py:205
  80.5 0.9 copy-start.1
  81.4 35.4 %all-to-all-start.2 = ((f32[32,3,3,8,256]{4,3,2,1,0:T(8,128)}), f32[32,3,3,8,256]{4,3,2,1,0:T(8,128)S(1)}, u32[]{:S(2)}, u32[]{:S(2)}) async-start(f32[32,3,3,8,256]{4,3,2,1,0:T(8,128)} %pad_maximum_fusion), calls=%async_computation.2 | async-start | bytes 4718592 | tf_op jit(solution)/shard_map/all_to_all | solution.py:210
  85.2 31.6 %copy-start = (s32[2]{0:T(128)S(1)}, s32[2]{0:T(128)}, u32[]{:S(2)}) copy-start(s32[2]{0:T(128)} %pad_add_fusion.place_ref) | copy-start | bytes 28
  85.2 4.4 %collective-permute-start = (f32[32,6,8,128]{3,2,1,0:T(8,128)}, f32[32,6,8,128]{3,2,1,0:T(8,128)S(1)}, u32[]{:S(2)}, u32[]{:S(2)}) collective-permute-start(f32[32,6,8,128]{3,2,1,0:T(8,128)} %copy-done.1), channel_id=1, source_target_pairs={{0,16},{16,0},{32,48},{48,32},{64,80},{80,64},{96,112},{112,96},{1... | collective-permute-start | bytes 2359304 | tf_op jit(solution)/shard_map/ppermute | solution.py:211
  89.6 0.9 copy-start.2

commit v9 on v8

--- a/solution.py
+++ b/solution.py
@@ -32,6 +32,7 @@
 
 def factor(block):
     groups = W // 8
+    half = groups // 2
     lane = lax.broadcasted_iota(jnp.int32, (8, W), 1)
     sub = lax.broadcasted_iota(jnp.int32, (8, W), 0)
     x = [block[8 * p : 8 * p + 8, :] for p in range(groups)]
@@ -40,7 +41,7 @@
     d = [lane_of(x[0], t) for t in range(8)]
     for p in range(groups):
         k = 8 * p
-        later = range(p + 1, groups)
+        later = range(p + 1, half if p < half else groups)
         c = {q: [lane_of(x[q], k + j) for j in range(8)] for q in later}
         ahead = [lane_of(x[p + 1], k + 8 + t) for t in range(8)] if later else None
         r = [row_of(x[p], j) for j in range(8)]
@@ -75,6 +76,13 @@
         upper.append(jnp.where(lane >= sub + k, u * root, 0.0))
         inverse.append(w * root)
         d = ahead
+        if p == half - 1:
+            done = jnp.concatenate([jnp.concatenate(upper, 0), jnp.concatenate(inverse, 0)], 1)
+            change = dot(done[:, 8 * half : W], done, 0, 0)
+            for q in range(half, groups):
+                rows = change[8 * (q - half) : 8 * (q - half) + 8]
+                x[q], v[q] = x[q] - rows[:, :W], v[q] - rows[:, W:]
+            d = [lane_of(x[half], 8 * half + t) for t in range(8)]
     return jnp.concatenate(upper, 0), jnp.concatenate(inverse, 0)
 
 

time: 127 us -> 126 us (level)
  Pallas kernels: 34.5 us -> 32.3 us
  waiting for transfers between devices: 14 us -> 15.7 us
    pallas_call x1, Pallas kernels: 26.2 us -> 24.1 us  [shards(): pl.pallas_call(lead_kernel, out_shape=[jax.ShapeDtypeStruct((N, N), f32),...]
    all_to_all x1, waiting for transfers between devices: 0.01 us -> 1.75 us  [shards(): tops = lax.all_to_all(tops, 'row', 0, 0)]
  transfers between devices with their start and end apart: 3 -> 3, of which waited for: 2 -> 3; matrix products, arithmetic and copies ran while one was open for 2% -> 2% of each run, Pallas kernels for 21% -> 19%
where the time goes in v9:
time: 126 us
  blocking collectives  53.7 us (43%)
  Pallas kernels  32.3 us (26%)
  starting transfers between devices  16.4 us (13%)
  waiting for transfers between devices  15.7 us (12%)
  local copies, waits for them, and re-layouts  5.32 us (4%)
  other arithmetic  2.28 us (2%)
    all_gather x1, blocking collectives, shards(): wide = lax.all_gather(pieces, 'col')  32.5 us
    pallas_call x1, Pallas kernels, shards(): pl.pallas_call(lead_kernel, out_shape=[jax.ShapeDtypeStruct((N, N), f32),...  24.1 us
    all_to_all x1, blocking collectives, shards(): pieces = lax.all_to_all(pieces, 'row', 0, 0)[:PANELS]  21.3 us
    all_to_all x1, waiting for transfers between devices, shards(): lead = lax.all_to_all(lead, 'row', 0, 0)  11.7 us
    all_to_all x1, starting transfers between devices, shards(): lead = lax.all_to_all(lead, 'row', 0, 0)  10.4 us
    pallas_call x1, Pallas kernels, shards(): pl.pallas_call(update_kernel, out_shape=jax.ShapeDtypeStruct((2, NB, NB),...  8.26 us
    all_to_all x1, starting transfers between devices, shards(): tops = lax.all_to_all(tops, 'row', 0, 0)  3.84 us
    unnamed x7, local copies, waits for them, and re-layouts  2.87 us
  transfers between devices with their start and end apart: 3, of which 3 were waited for; matrix products, arithmetic and copies ran while one was open for 2% of the time, Pallas kernels for 19%

profile of v9, /device:TPU:1, one launch (start us, length us, event | category | flops | bytes accessed | tf_op | source)
XLA Modules:
  0.0 125.8 jit_solution(17756214309690749220)
XLA Ops:
  0.0 1.1 copy.28
  1.1 0.1 copy.27
  1.1 21.3 %all_to_all.15 = f32[32,2,8,256]{3,2,1,0:T(8,128)S(1)} all-to-all(f32[32,2,8,256]{3,2,1,0:T(8,128)S(1)} %bitcast.41), channel_id=1, replica_groups=mesh['row'=32,'col'=16] {'row'}, dimensions={0} | all-to-all | bytes 1048576 | tf_op jit(solution)/shard_map/all_to_all | solution.py:208
  22.4 32.5 %all-gather = f32[48,2,8,256]{3,2,1,0:T(8,128)S(1)} all-gather(f32[3,2,8,256]{3,2,1,0:T(8,128)S(1)} %slice.16), channel_id=2, replica_groups=mesh['row'=32,'col'=16] {'col'}, dimensions={0}, use_global_device_ids=true | all-gather | bytes 835584 | tf_op jit(solution)/shard_map/all_gather | solution.py:209
  54.9 1.0 broadcast_in_dim.6
  55.8 10.4 %all-to-all-start.1 = ((f32[32,6,8,128]{3,2,1,0:T(8,128)}), f32[32,6,8,128]{3,2,1,0:T(8,128)S(1)}, u32[]{:S(2)}, u32[]{:S(2)}) async-start(f32[32,6,8,128]{3,2,1,0:T(8,128)} %bitcast.10), calls=%async_computation.1 | async-start | bytes 1572864 | tf_op jit(solution)/shard_map/all_to_all | solution.py:213
  66.2 0.7 pad_add_fusion.place_ref
  66.9 0.1 copy.18
  66.9 0.2 broadcast_in_dim.7
  67.1 1.6 %pad_maximum_fusion = f32[32,3,3,8,256]{4,3,2,1,0:T(8,128)} fusion(f32[32,3,1,8,256]{4,3,2,1,0:T(8,128)S(1)} %bitcast.40, f32[32,3,2,8,256]{4,3,2,1,0:T(8,128)S(1)} %broadcast_in_dim.7), kind=kLoop, calls=%fused_computation | loop fusion | flops 589824 | bytes 4718592 | tf_op jit(solution)/shard_map/concatenate | solution.py:215
  68.8 11.7 %all-to-all-done.1.mine_ref = f32[32,6,8,128]{3,2,1,0:T(8,128)S(1)} async-done(((f32[32,6,8,128]{3,2,1,0:T(8,128)}), f32[32,6,8,128]{3,2,1,0:T(8,128)S(1)}, u32[]{:S(2)}, u32[]{:S(2)}) %all-to-all-start.1) | async-done | bytes 786464 | tf_op jit(solution)/shard_map/all_to_all | solution.py:213
  80.5 0.0 copy-start.1
  80.5 0.9 copy-done.1
  81.4 3.8 %all-to-all-start.2 = ((f32[32,3,3,8,256]{4,3,2,1,0:T(8,128)}), f32[32,3,3,8,256]{4,3,2,1,0:T(8,128)S(1)}, u32[]{:S(2)}, u32[]{:S(2)}) async-start(f32[32,3,3,8,256]{4,3,2,1,0:T(8,128)} %pad_maximum_fusion), calls=%async_computation.2 | async-start | bytes 4718592 | tf_op jit(solution)/shard_map/all_to_all | solution.py:218
  85.2 0.0 copy-start
  85.2 2.1 %collective-permute-start = (f32[32,6,8,128]{3,2,1,0:T(8,128)}, f32[32,6,8,128]{3,2,1,0:T(8,128)S(1)}, u32[]{:S(2)}, u32[]{:S(2)}) collective-permute-start(f32[32,6,8,128]{3,2,1,0:T(8,128)} %copy-done.1), channel_id=1, source_target_pairs={{0,16},{16,0},{32,48},{48,32},{64,80},{80,64},{96,112},{112,96},{1... | collective-permute-start | bytes 2359304 | tf_op jit(solution)/shard_map/ppermute | solution.py:219
  87.4 2.3 %collective-permute-done.other_ref = f32[32,6,8,128]{3,2,1,0:T(8,128)S(1)} collective-permute-done((f32[32,6,8,128]{3,2,1,0:T(8,128)}, f32[32,6,8,128]{3,2,1,0:T(8,128)S(1)}, u32[]{:S(2)}, u32[]{:S(2)}) %collective-permute-start) | collective-permute-done | bytes 786464 | tf_op jit(solution)/shard_map/ppermute | solution.py:219
  89.6 0.0 copy-start.2
  89.6 0.9 copy-done.2
  90.5 24.1 %shard_map.17 = (f32[768,768]{1,0:T(8,128)}, f32[768,256]{1,0:T(8,128)}) custom-call(s32[2]{0:T(128)} %pad_add_fusion.place_ref, f32[32,6,8,128]{3,2,1,0:T(8,128)} %copy-done.1, f32[32,6,8,128]{3,2,1,0:T(8,128)} %copy-done.2), custom_call_target="tpu_custom_call" | custom-call | flops 2147483648 | bytes 104857600 | tf_op jit(solution)/shard_map/pallas_call | solution.py:222
  114.6 1.8 %all-to-all-done.2.t_ref = f32[32,3,3,8,256]{4,3,2,1,0:T(8,128)S(1)} async-done(((f32[32,3,3,8,256]{4,3,2,1,0:T(8,128)}), f32[32,3,3,8,256]{4,3,2,1,0:T(8,128)S(1)}, u32[]{:S(2)}, u32[]{:S(2)}) %all-to-all-start.2) | async-done | bytes 2359328 | tf_op jit(solution)/shard_map/all_to_all | solution.py:218
  116.3 0.0 copy-done
  116.3 8.3 %shard_map.18 = f32[2,256,256]{2,1,0:T(8,128)S(1)} custom-call(s32[2]{0:T(128)S(1)} %copy-done, f32[32,3,3,8,256]{4,3,2,1,0:T(8,128)S(1)} %all-to-all-done.2.t_ref, f32[768,768]{1,0:T(8,128)} %get-tuple-element.13.upper_ref, f32[768,256]{1,0:T(8,128)} %get-tuple-element.14.inverse_ref, f32[2,256,256]{2,1,0:T(8,128)S(1)} %bitcast.34), custom_call_target="tpu_custom_call" | custom-call | flops 2147483648 | bytes 8388608 | tf_op jit(solution)/shard_map/pallas_call | solution.py:238
  124.6 1.2 copy.19
  (4 shorter events, 0.0 us)
Async XLA Ops:
  55.8 24.6 %all-to-all-start.1 = ((f32[32,6,8,128]{3,2,1,0:T(8,128)}), f32[32,6,8,128]{3,2,1,0:T(8,128)S(1)}, u32[]{:S(2)}, u32[]{:S(2)}) async-start(f32[32,6,8,128]{3,2,1,0:T(8,128)} %bitcast.10), calls=%async_computation.1 | async-start | bytes 1572864 | tf_op jit(solution)/shard_map/all_to_all | solution.py:213
  80.5 0.9 copy-start.1
  81.4 35.0 %all-to-all-start.2 = ((f32[32,3,3,8,256]{4,3,2,1,0:T(8,128)}), f32[32,3,3,8,256]{4,3,2,1,0:T(8,128)S(1)}, u32[]{:S(2)}, u32[]{:S(2)}) async-start(f32[32,3,3,8,256]{4,3,2,1,0:T(8,128)} %pad_maximum_fusion), calls=%async_computation.2 | async-start | bytes 4718592 | tf_op jit(solution)/shard_map/all_to_all | solution.py:218
  85.2 31.1 %copy-start = (s32[2]{0:T(128)S(1)}, s32[2]{0:T(128)}, u32[]{:S(2)}) copy-start(s32[2]{0:T(128)} %pad_add_fusion.place_ref) | copy-start | bytes 28
  85.2 4.4 %collective-permute-start = (f32[32,6,8,128]{3,2,1,0:T(8,128)}, f32[32,6,8,128]{3,2,1,0:T(8,128)S(1)}, u32[]{:S(2)}, u32[]{:S(2)}) collective-permute-start(f32[32,6,8,128]{3,2,1,0:T(8,128)} %copy-done.1), channel_id=1, source_target_pairs={{0,16},{16,0},{32,48},{48,32},{64,80},{80,64},{96,112},{112,96},{1... | collective-permute-start | bytes 2359304 | tf_op jit(solution)/shard_map/ppermute | solution.py:219
  89.6 0.9 copy-start.2

commit v10 on v9

--- a/solution.py
+++ b/solution.py
@@ -148,7 +148,7 @@
         v_ref[m : m + W, 0:W] = -dot(v_ref[m : m + W, W:NB], cross)
 
 
-def update_kernel(place_ref, t_ref, upper_ref, inverse_ref, m_ref, o_ref, w_ref, u_ref, v_ref, sems):
+def update_kernel(place_ref, t_ref, upper_ref, inverse_ref, mine_ref, o_ref, w_ref, u_ref, v_ref, m_ref, sems, late):
     i, c = place_ref[0], place_ref[1]
     own = pl.ds(pl.multiple_of(jnp.minimum(i, PANELS - 1) * NB, NB), NB)
     factors = pltpu.make_async_copy(upper_ref.at[:, own], u_ref.at[:, 0:NB], sems.at[1, 0])
@@ -163,6 +163,9 @@
         for arrival in arrivals[k]:
             arrival.start()
 
+    matrix = pltpu.make_async_copy(mine_ref, m_ref, late)
+    matrix.start()
+
     @pl.when(i < PANELS)
     def _():
         factors.start()
@@ -182,6 +185,7 @@
         w_ref[:, 2 * NB :] = u_ref[:, 0:NB]
 
     product = dot(w_ref[:, 2 * NB :], w_ref[:, : 2 * NB], 0, 0)
+    matrix.wait()
     keep = i >= PANELS
     o_ref[1] = jnp.where(keep, m_ref[1] - product[:, NB:], 0.0)
 
@@ -238,17 +242,19 @@
     out = pl.pallas_call(
         update_kernel,
         out_shape=jax.ShapeDtypeStruct((2, NB, NB), f32),
-        in_specs=[pl.BlockSpec(memory_space=pltpu.SMEM), vmem, hbm, hbm, vmem],
+        in_specs=[pl.BlockSpec(memory_space=pltpu.SMEM), vmem, hbm, hbm, hbm],
         out_specs=vmem,
         scratch_shapes=[
             pltpu.VMEM((N, 3 * NB), f32),
             pltpu.VMEM((N, N), f32),
             pltpu.VMEM((N, NB), f32),
+            pltpu.VMEM((2, NB, NB), f32),
             pltpu.SemaphoreType.DMA((2, PANELS)),
+            pltpu.SemaphoreType.DMA,
         ],
         compiler_params=pltpu.CompilerParams(vmem_limit_bytes=24 << 20),
         cost_estimate=pl.CostEstimate(flops=2 << 30, bytes_accessed=8 << 20, transcendentals=0),
-    )(place, tops, pltpu.with_memory_space_constraint(upper, pltpu.HBM), pltpu.with_memory_space_constraint(inverse, pltpu.HBM), mine)
+    )(place, tops, pltpu.with_memory_space_constraint(upper, pltpu.HBM), pltpu.with_memory_space_constraint(inverse, pltpu.HBM), pltpu.with_memory_space_constraint(mine, pltpu.HBM))
     return out.transpose(1, 0, 2)[None]
 
 

time: 126 us -> 125 us (level)
    unnamed x7 -> x9, local copies, waits for them, and re-layouts: 2.87 us -> 1.98 us
where the time goes in v10:
time: 125 us
  blocking collectives  53.7 us (43%)
  Pallas kernels  32.3 us (26%)
  starting transfers between devices  16.4 us (13%)
  waiting for transfers between devices  15.7 us (13%)
  local copies, waits for them, and re-layouts  4.43 us (4%)
  other arithmetic  2.24 us (2%)
    all_gather x1, blocking collectives, shards(): wide = lax.all_gather(pieces, 'col')  32.5 us
    pallas_call x1, Pallas kernels, shards(): pl.pallas_call(lead_kernel, out_shape=[jax.ShapeDtypeStruct((N, N), f32),...  24.1 us
    all_to_all x1, blocking collectives, shards(): pieces = lax.all_to_all(pieces, 'row', 0, 0)[:PANELS]  21.3 us
    all_to_all x1, waiting for transfers between devices, shards(): lead = lax.all_to_all(lead, 'row', 0, 0)  11.7 us
    all_to_all x1, starting transfers between devices, shards(): lead = lax.all_to_all(lead, 'row', 0, 0)  10.4 us
    pallas_call x1, Pallas kernels, shards(): pl.pallas_call(update_kernel, out_shape=jax.ShapeDtypeStruct((2, NB, NB),...  8.28 us
    all_to_all x1, starting transfers between devices, shards(): tops = lax.all_to_all(tops, 'row', 0, 0)  3.85 us
  transfers between devices with their start and end apart: 3, of which 3 were waited for; matrix products, arithmetic and copies ran while one was open for 2% of the time, Pallas kernels for 19%

profile of v10, /device:TPU:1, one launch (start us, length us, event | category | flops | bytes accessed | tf_op | source)
XLA Modules:
  0.0 124.9 jit_solution(7873466726264659868)
XLA Ops:
  0.0 1.1 copy.28
  1.1 0.0 copy-start.1
  1.1 0.1 copy.27
  1.2 21.3 %all_to_all.15 = f32[32,2,8,256]{3,2,1,0:T(8,128)S(1)} all-to-all(f32[32,2,8,256]{3,2,1,0:T(8,128)S(1)} %bitcast.41), channel_id=1, replica_groups=mesh['row'=32,'col'=16] {'row'}, dimensions={0} | all-to-all | bytes 1048576 | tf_op jit(solution)/shard_map/all_to_all | solution.py:212
  22.4 32.5 %all-gather = f32[48,2,8,256]{3,2,1,0:T(8,128)S(1)} all-gather(f32[3,2,8,256]{3,2,1,0:T(8,128)S(1)} %slice.16), channel_id=2, replica_groups=mesh['row'=32,'col'=16] {'col'}, dimensions={0}, use_global_device_ids=true | all-gather | bytes 835584 | tf_op jit(solution)/shard_map/all_gather | solution.py:213
  54.9 1.0 broadcast_in_dim.6
  55.8 0.0 copy-done.1
  55.8 10.4 %all-to-all-start.1 = ((f32[32,6,8,128]{3,2,1,0:T(8,128)}), f32[32,6,8,128]{3,2,1,0:T(8,128)S(1)}, u32[]{:S(2)}, u32[]{:S(2)}) async-start(f32[32,6,8,128]{3,2,1,0:T(8,128)} %bitcast.10), calls=%async_computation.1 | async-start | bytes 1572864 | tf_op jit(solution)/shard_map/all_to_all | solution.py:217
  66.3 0.6 pad_add_fusion.place_ref
  66.9 0.1 copy.18
  66.9 0.2 broadcast_in_dim.7
  67.1 1.6 %pad_maximum_fusion = f32[32,3,3,8,256]{4,3,2,1,0:T(8,128)} fusion(f32[32,3,1,8,256]{4,3,2,1,0:T(8,128)S(1)} %bitcast.38, f32[32,3,2,8,256]{4,3,2,1,0:T(8,128)S(1)} %broadcast_in_dim.7), kind=kLoop, calls=%fused_computation | loop fusion | flops 589824 | bytes 4718592 | tf_op jit(solution)/shard_map/concatenate | solution.py:219
  68.7 11.7 %all-to-all-done.1.mine_ref = f32[32,6,8,128]{3,2,1,0:T(8,128)S(1)} async-done(((f32[32,6,8,128]{3,2,1,0:T(8,128)}), f32[32,6,8,128]{3,2,1,0:T(8,128)S(1)}, u32[]{:S(2)}, u32[]{:S(2)}) %all-to-all-start.1) | async-done | bytes 786464 | tf_op jit(solution)/shard_map/all_to_all | solution.py:217
  80.5 0.0 copy-start.2
  80.5 3.8 %all-to-all-start.2 = ((f32[32,3,3,8,256]{4,3,2,1,0:T(8,128)}), f32[32,3,3,8,256]{4,3,2,1,0:T(8,128)S(1)}, u32[]{:S(2)}, u32[]{:S(2)}) async-start(f32[32,3,3,8,256]{4,3,2,1,0:T(8,128)} %pad_maximum_fusion), calls=%async_computation.2 | async-start | bytes 4718592 | tf_op jit(solution)/shard_map/all_to_all | solution.py:222
  84.3 0.0 copy-start
  84.3 2.1 %collective-permute-start = (f32[32,6,8,128]{3,2,1,0:T(8,128)S(1)}, f32[32,6,8,128]{3,2,1,0:T(8,128)S(1)}, u32[]{:S(2)}, u32[]{:S(2)}) collective-permute-start(f32[32,6,8,128]{3,2,1,0:T(8,128)S(1)} %all-to-all-done.1.mine_ref), channel_id=1, source_target_pairs={{0,16},{16,0},{32,48},{48,32},{64,80},{80,64},{96,112},{112,96},{1... | collective-permute-start | bytes 2359304 | tf_op jit(solution)/shard_map/ppermute | solution.py:223
  86.5 2.0 %collective-permute-done.other_ref = f32[32,6,8,128]{3,2,1,0:T(8,128)S(1)} collective-permute-done((f32[32,6,8,128]{3,2,1,0:T(8,128)S(1)}, f32[32,6,8,128]{3,2,1,0:T(8,128)S(1)}, u32[]{:S(2)}, u32[]{:S(2)}) %collective-permute-start) | collective-permute-done | bytes 786464 | tf_op jit(solution)/shard_map/ppermute | solution.py:223
  88.5 0.0 copy-done.2
  88.5 0.0 copy-start.3
  88.5 0.9 copy-done.3
  89.4 24.1 %shard_map.17 = (f32[768,768]{1,0:T(8,128)}, f32[768,256]{1,0:T(8,128)}) custom-call(s32[2]{0:T(128)} %pad_add_fusion.place_ref, f32[32,6,8,128]{3,2,1,0:T(8,128)} %copy-done.2, f32[32,6,8,128]{3,2,1,0:T(8,128)} %copy-done.3), custom_call_target="tpu_custom_call" | custom-call | flops 2147483648 | bytes 104857600 | tf_op jit(solution)/shard_map/pallas_call | solution.py:226
  113.5 2.0 %all-to-all-done.2.t_ref = f32[32,3,3,8,256]{4,3,2,1,0:T(8,128)S(1)} async-done(((f32[32,3,3,8,256]{4,3,2,1,0:T(8,128)}), f32[32,3,3,8,256]{4,3,2,1,0:T(8,128)S(1)}, u32[]{:S(2)}, u32[]{:S(2)}) %all-to-all-start.2) | async-done | bytes 2359328 | tf_op jit(solution)/shard_map/all_to_all | solution.py:222
  115.5 0.0 copy-done
  115.5 8.3 %shard_map.18 = f32[2,256,256]{2,1,0:T(8,128)S(1)} custom-call(s32[2]{0:T(128)S(1)} %copy-done, f32[32,3,3,8,256]{4,3,2,1,0:T(8,128)S(1)} %all-to-all-done.2.t_ref, f32[768,768]{1,0:T(8,128)} %get-tuple-element.13.upper_ref, f32[768,256]{1,0:T(8,128)} %get-tuple-element.14.inverse_ref, f32[2,256,256]{2,1,0:T(8,128)} %bitcast.40), custom_call_target="tpu_custom_call" | custom-call | flops 2147483648 | bytes 8388608 | tf_op jit(solution)/shard_map/pallas_call | solution.py:242
  123.7 1.2 copy.19
  (4 shorter events, 0.0 us)
Async XLA Ops:
  1.1 54.8 %copy-start.1 = (f32[1,256,2,256]{3,1,2,0:T(8,128)}, f32[1,256,2,256]{3,1,2,0:T(8,128)S(1)}, u32[]{:S(2)}) copy-start(f32[1,256,2,256]{3,1,2,0:T(8,128)S(1)} %copy.28) | copy-start | bytes 1572868
  55.8 24.6 %all-to-all-start.1 = ((f32[32,6,8,128]{3,2,1,0:T(8,128)}), f32[32,6,8,128]{3,2,1,0:T(8,128)S(1)}, u32[]{:S(2)}, u32[]{:S(2)}) async-start(f32[32,6,8,128]{3,2,1,0:T(8,128)} %bitcast.10), calls=%async_computation.1 | async-start | bytes 1572864 | tf_op jit(solution)/shard_map/all_to_all | solution.py:217
  80.5 8.1 %copy-start.2 = (f32[32,6,8,128]{3,2,1,0:T(8,128)}, f32[32,6,8,128]{3,2,1,0:T(8,128)S(1)}, u32[]{:S(2)}) copy-start(f32[32,6,8,128]{3,2,1,0:T(8,128)S(1)} %all-to-all-done.1.mine_ref) | copy-start | bytes 2359300
  80.5 35.0 %all-to-all-start.2 = ((f32[32,3,3,8,256]{4,3,2,1,0:T(8,128)}), f32[32,3,3,8,256]{4,3,2,1,0:T(8,128)S(1)}, u32[]{:S(2)}, u32[]{:S(2)}) async-start(f32[32,3,3,8,256]{4,3,2,1,0:T(8,128)} %pad_maximum_fusion), calls=%async_computation.2 | async-start | bytes 4718592 | tf_op jit(solution)/shard_map/all_to_all | solution.py:222
  84.3 31.1 %copy-start = (s32[2]{0:T(128)S(1)}, s32[2]{0:T(128)}, u32[]{:S(2)}) copy-start(s32[2]{0:T(128)} %pad_add_fusion.place_ref) | copy-start | bytes 28
  84.3 4.2 %collective-permute-start = (f32[32,6,8,128]{3,2,1,0:T(8,128)S(1)}, f32[32,6,8,128]{3,2,1,0:T(8,128)S(1)}, u32[]{:S(2)}, u32[]{:S(2)}) collective-permute-start(f32[32,6,8,128]{3,2,1,0:T(8,128)S(1)} %all-to-all-done.1.mine_ref), channel_id=1, source_target_pairs={{0,16},{16,0},{32,48},{48,32},{64,80},{80,64},{96,112},{112,96},{1... | collective-permute-start | bytes 2359304 | tf_op jit(solution)/shard_map/ppermute | solution.py:223
  88.5 0.9 copy-start.3
